TPU v7x, 32 devices: a whole 2x2x4 slice. The times are simulated.
32 devices in a mesh: role: 2 (over core), dev: 16 (over z, y, x).
Axes of the slice: x: 2, y: 2, z: 4, core: 2. Of those that a mesh axis runs over, the one named last changes fastest.
Arguments:
- positions: float32 [256, 3, 512], P(('role', 'dev')), may hold values from -1 to 1
- normals: float32 [256, 3, 512], P(('role', 'dev')), may hold values from -3.6 to 3.6
- panel_areas: float32 [256, 512], P(('role', 'dev')), may hold values from 0.005 to 0.05
- panel_counts: int32 [256], P(('role', 'dev')), may hold values from 128 to 512, as said below
- near_lists: int32 [256, 6], P(('role', 'dev')), may hold values from 0 to 255, as said below
- near_counts: int32 [256], P(('role', 'dev')), may hold values from 1 to 6
- leaf_lists: int32 [256, 16], P(('role', 'dev')), may hold values from 0 to 255, as said below
- leaf_kinds: int32 [256, 16], P(('role', 'dev')), may hold values from 0 to 7
- group_lists: int32 [32, 16], P(('role', 'dev')), may hold values from 0 to 31
- group_kinds: int32 [32, 16], P(('role', 'dev')), may hold values from 0 to 7
- block_inverse: bfloat16 [256, 512, 512], P(('role', 'dev')), may hold values from -1 to 3
- moment_maps: bfloat16 [256, 256, 512], P(('role', 'dev')), may hold values from -0.25 to 0.25
- up_operators: bfloat16 [8, 256, 256], replicated, may hold values from -0.125 to 0.125
- far_operators: bfloat16 [2, 8, 256, 256], replicated, may hold values from -0.09375 to 0.09375
- krylov_basis: float32 [8, 256, 512], P(None, ('role', 'dev')), may hold values from -64 to 64, as said below
Outputs:
- next_vector: float32 [256, 512], P(('role', 'dev'))
- hessenberg_column: float32 [9], replicated
Inputs may be any that keep to these rules, and one draw needn't show every extreme that they name: `panel_counts`: some cluster has all 512 panels live. `near_lists`: ids of clusters held by the devices at most 3 places from the cluster's own device along role+dev; entries may repeat. `leaf_lists`: ids of clusters held by the devices at most 3 places from the cluster's own device along role+dev; entries may repeat. `krylov_basis`: the vectors are orthonormal under the mean over all 131072 entries, and zero on panels that are not live.
All inputs are finite; a program needn't handle non-finite values.
Results may differ from a plain program's by a relative error of at most 0.0044.
Values may be sent and summed in bfloat16 or wider, within the bound.
A program may use at most 64 MiB of HBM per device.

v0:
```python
import jax
import jax.numpy as jnp
from jax import lax
from jax.sharding import PartitionSpec as P

RADIUS = 3


SOFTEN = 0.01
EPSILON = 1e-06
HIGH = lax.Precision.HIGHEST


def passed_along(block, axis, distance):
    devices = range(lax.axis_size(axis))
    route = [(i - distance, i) for i in devices if i - distance in devices]
    return lax.ppermute(block, axis, route)


def near_cluster(operands):
    target, sources = operands
    square = jnp.full((sources.shape[0], target.shape[1], sources.shape[2]), SOFTEN, jnp.float32)
    projected = jnp.zeros((sources.shape[0], target.shape[1], sources.shape[2]), jnp.float32)
    for component in range(3):
        offsets = target[component][None, :, None] - sources[:, component][:, None, :]
        square = square + offsets * offsets
        projected = projected + offsets * sources[:, 3 + component][:, None, :]
    inverse = lax.rsqrt(square)
    return jnp.sum(projected * inverse * inverse * inverse, axis=(0, 2))


def translate(chosen, kind_ids, operators):
    onehot = (
        kind_ids[:, :, None] == jnp.arange(operators.shape[0], dtype=jnp.int32)[None, None, :]
    ).astype(jnp.float32)
    summed = jnp.einsum("gno,gnc->goc", onehot, chosen, precision=HIGH)
    return jnp.einsum("goc,oqc->gq", summed, operators, precision=HIGH)


def near_rims(block):
    lower = [passed_along(block, ("role", "dev"), distance) for distance in range(RADIUS, 0, -1)]
    upper = [passed_along(block, ("role", "dev"), -distance) for distance in range(1, RADIUS + 1)]
    return jnp.concatenate(lower + [block] + upper, axis=0)


def moment_rims(block):
    lower = [passed_along(block, ("role", "dev"), distance) for distance in range(RADIUS, 0, -1)]
    upper = [passed_along(block, ("role", "dev"), -distance) for distance in range(1, RADIUS + 1)]
    return jnp.concatenate(lower + [block] + upper, axis=0)


def shards(
    positions,
    normals,
    panel_areas,
    panel_counts,
    near_lists,
    near_counts,
    leaf_lists,
    leaf_kinds,
    group_lists,
    group_kinds,
    block_inverse,
    moment_maps,
    up_operators,
    far_operators,
    krylov_basis,
):
    local_count = positions.shape[0]
    panels = positions.shape[2]
    coeff_count = moment_maps.shape[1]
    own_index = lax.axis_index(("role", "dev"))
    devices_all = lax.axis_size(("role", "dev"))
    first_cluster = (own_index - RADIUS) * local_count
    live = (
        lax.broadcasted_iota(jnp.int32, (local_count, panels), 1) < panel_counts[:, None]
    ).astype(jnp.float32)
    current = krylov_basis[-1].astype(jnp.bfloat16)
    density = jnp.einsum("cij,cj->ci", block_inverse, current, preferred_element_type=jnp.float32)
    density = (live * density).astype(jnp.bfloat16)
    density_wide = density.astype(jnp.float32)
    weighted = (panel_areas * density_wide)[:, None, :] * normals
    sources = jnp.concatenate([positions, weighted], axis=1)
    moments = jnp.einsum(
        "cqp,cp->cq", moment_maps, density, preferred_element_type=jnp.float32
    ).astype(jnp.bfloat16)
    near_window = near_rims(sources)
    moment_window = moment_rims(moments).astype(jnp.float32)
    own_ids = own_index * local_count + lax.broadcasted_iota(jnp.int32, (local_count, 1), 0)
    slot_ids = jnp.concatenate([own_ids, near_lists], axis=1) - first_cluster
    slot_live = (lax.broadcasted_iota(jnp.int32, slot_ids.shape, 1) <= near_counts[:, None]).astype(
        jnp.float32
    )
    gathered = near_window[slot_ids] * slot_live[:, :, None, None]
    near_field = lax.map(near_cluster, (positions, gathered))
    groups_here = local_count // 8
    children = moments.reshape(groups_here, 8, coeff_count)
    group_moments = jnp.einsum(
        "gkc,kqc->gq", children, up_operators, preferred_element_type=jnp.float32
    )
    all_groups = lax.all_gather(group_moments, ("role", "dev"), axis=0, tiled=True)
    far_wide = far_operators.astype(jnp.float32)
    group_local = translate(all_groups[group_lists], group_kinds, far_wide[1]).astype(jnp.bfloat16)
    downward = jnp.einsum(
        "gq,kqc->gkc", group_local, up_operators, preferred_element_type=jnp.float32
    ).reshape(local_count, coeff_count)
    leaf_local = (
        translate(moment_window[leaf_lists - first_cluster], leaf_kinds, far_wide[0]) + downward
    ).astype(jnp.bfloat16)
    far_field = jnp.einsum(
        "cqp,cq->cp", moment_maps, leaf_local, preferred_element_type=jnp.float32
    )
    image = live * (0.5 * density_wide + near_field + far_field)
    inverse_rows = 1.0 / (devices_all * local_count * panels)
    projected = jnp.einsum("kcp,cp->k", krylov_basis, image, precision=HIGH)
    totals, square = lax.psum((projected, jnp.sum(image * image)), ("role", "dev"))
    coeffs = totals * inverse_rows
    remainder = image - jnp.einsum("k,kcp->cp", coeffs, krylov_basis, precision=HIGH)
    energy = square * inverse_rows - jnp.sum(coeffs * coeffs)
    height = jnp.sqrt(energy + EPSILON)
    return (remainder / height, jnp.concatenate([coeffs, height[None]]))


def solution(mesh):
    return jax.shard_map(
        shards,
        mesh=mesh,
        in_specs=(
            P(("role", "dev"), None, None),
            P(("role", "dev"), None, None),
            P(("role", "dev"), None),
            P(("role", "dev")),
            P(("role", "dev"), None),
            P(("role", "dev")),
            P(("role", "dev"), None),
            P(("role", "dev"), None),
            P(("role", "dev"), None),
            P(("role", "dev"), None),
            P(("role", "dev"), None, None),
            P(("role", "dev"), None, None),
            P(),
            P(),
            P(None, ("role", "dev"), None),
        ),
        out_specs=(P(("role", "dev"), None), P()),
        check_vma=False,
    )
```

profile of v0, /device:TPU:0, one launch (start us, length us, event | category | flops | bytes accessed | tf_op | source)
XLA Modules:
  0.0 222.1 jit_solution(16200773161611633112)
XLA Ops:
  0.7 0.9 fusion.31
  1.6 3.5 %fusion.28 = bf16[8,1,512]{2,1,0:T(2,128)(2,1)S(1)} fusion(bf16[8,512,512]{2,1,0:T(8,128)(2,1)} %param.27, bf16[8,512,1]{1,0,2:T(8,128)(2,1)S(1)} %fusion.31), kind=kOutput, calls=%fused_computation.76 | convolution fusion | flops 4194304 | bytes 4210688 | tf_op jit(solution)/shard_map/cij,cj->ci/dot_general | solution.py:79
  5.1 0.1 convert_multiply_fusion
  5.2 0.6 fusion.26
  5.9 5.8 %collective-permute-start.6 = (bf16[8,256]{1,0:T(8,128)(2,1)S(1)}, bf16[8,256]{1,0:T(8,128)(2,1)S(1)}, u32[]{:S(2)}, u32[]{:S(2)}) collective-permute-start(bf16[8,256]{1,0:T(8,128)(2,1)S(1)} %bitcast.130), channel_id=1, source_target_pairs={{0,3},{1,4},{2,5},{3,6},{4,7},{5,8},{6,9},{7,10},{8,11},{9,12},{10... | collective-permute-start | bytes 12296 | tf_op jit(solution)/shard_map/ppermute | solution.py:17
  11.7 3.4 %collective-permute-start.7 = (bf16[8,256]{1,0:T(8,128)(2,1)S(1)}, bf16[8,256]{1,0:T(8,128)(2,1)S(1)}, u32[]{:S(2)}, u32[]{:S(2)}) collective-permute-start(bf16[8,256]{1,0:T(8,128)(2,1)S(1)} %bitcast.131), channel_id=1, source_target_pairs={{0,2},{1,3},{2,4},{3,5},{4,6},{5,7},{6,8},{7,9},{8,10},{9,11},{10,... | collective-permute-start | bytes 12296 | tf_op jit(solution)/shard_map/ppermute | solution.py:17
  15.1 2.5 %collective-permute-start.8 = (bf16[8,256]{1,0:T(8,128)(2,1)S(1)}, bf16[8,256]{1,0:T(8,128)(2,1)S(1)}, u32[]{:S(2)}, u32[]{:S(2)}) collective-permute-start(bf16[8,256]{1,0:T(8,128)(2,1)S(1)} %bitcast.132), channel_id=1, source_target_pairs={{0,1},{1,2},{2,3},{3,4},{4,5},{5,6},{6,7},{7,8},{8,9},{9,10},{10,1... | collective-permute-start | bytes 12296 | tf_op jit(solution)/shard_map/ppermute | solution.py:17
  17.6 1.3 collective-permute-start.9
  18.9 1.3 collective-permute-start.10
  20.3 0.1 reshape.156
  20.4 0.4 convolution_bitcast_fusion.2
  20.8 67.9 %all-gather.1 = f32[32,1,256]{2,1,0:T(1,128)S(1)} all-gather(f32[1,1,256]{2,1,0:T(1,128)S(1)} %convolution_bitcast_fusion.2), channel_id=2, replica_groups=mesh['role'=2,'dev'=16] {'role','dev'}, dimensions={0}, use_global_device_ids=true | all-gather | bytes 33792 | tf_op jit(solution)/shard_map/all_gather | solution.py:101
  88.6 0.6 gather_fusion.2
  89.2 0.1 convolution_bitcast_fusion
  89.3 2.1 fusion.10
  91.5 0.2 fusion.44
  91.8 0.1 copy.28
  91.9 0.1 compare_select_fusion.1
  92.0 0.1 reshape.148
  92.3 1.3 collective-permute-start.11
  93.6 5.5 %collective-permute-start = (f32[8,6,512]{2,1,0:T(8,128)S(1)}, f32[8,6,512]{2,1,0:T(8,128)S(1)}, u32[]{:S(2)}, u32[]{:S(2)}) collective-permute-start(f32[8,6,512]{2,1,0:T(8,128)S(1)} %pad_maximum_fusion), channel_id=1, source_target_pairs={{0,3},{1,4},{2,5},{3,6},{4,7},{5,8},{6,9},{7,10},{8,11},{9,12},{10... | collective-permute-start | bytes 294920 | tf_op jit(solution)/shard_map/ppermute | solution.py:17
  99.1 1.5 collective-permute-start.1
  100.7 2.8 %collective-permute-start.2 = (f32[8,6,512]{2,1,0:T(8,128)S(1)}, f32[8,6,512]{2,1,0:T(8,128)S(1)}, u32[]{:S(2)}, u32[]{:S(2)}) collective-permute-start(f32[8,6,512]{2,1,0:T(8,128)S(1)} %pad_maximum_fusion), channel_id=1, source_target_pairs={{0,1},{1,2},{2,3},{3,4},{4,5},{5,6},{6,7},{7,8},{8,9},{9,10},{10,1... | collective-permute-start | bytes 294920 | tf_op jit(solution)/shard_map/ppermute | solution.py:17
  103.5 1.3 collective-permute-start.3
  104.9 1.3 collective-permute-start.4
  106.2 0.8 gather_fusion.1
  107.0 0.1 fusion.19
  107.2 2.1 fusion.9
  109.3 0.4 fusion.32
  109.7 1.3 collective-permute-start.5
  111.0 0.7 constant_dynamic-update-slice_fusion.6
  111.7 0.7 constant_dynamic-update-slice_fusion.5
  112.3 0.7 constant_dynamic-update-slice_fusion.4
  113.0 0.7 constant_dynamic-update-slice_fusion.3
  113.7 0.7 constant_dynamic-update-slice_fusion.2
  114.3 0.7 constant_dynamic-update-slice_fusion.1
  115.0 4.3 %collective-permute-done.5 = f32[8,6,512]{2,1,0:T(8,128)S(1)} collective-permute-done((f32[8,6,512]{2,1,0:T(8,128)S(1)}, f32[8,6,512]{2,1,0:T(8,128)S(1)}, u32[]{:S(2)}, u32[]{:S(2)}) %collective-permute-start.5) | collective-permute-done | bytes 98336 | tf_op jit(solution)/shard_map/ppermute | solution.py:17
  119.3 0.7 constant_dynamic-update-slice_fusion
  119.9 1.8 gather_fusion
  121.7 1.3 copy_multiply_fusion
  123.0 48.8 %while.11 = (s32[]{:T(128)}, f32[8,512]{1,0:T(8,128)S(1)}, f32[8,3,512]{2,0,1:T(8,128)S(1)}, f32[8,7,6,512]{3,1,2,0:T(8,128)}) while((s32[]{:T(128)}, f32[8,512]{1,0:T(8,128)S(1)}, f32[8,3,512]{2,0,1:T(8,128)S(1)}, f32[8,7,6,512]{3,1,2,0:T(8,128)}) %tuple.44), condition=%wide.region_2.3_spmd.clone, body=%wide.region_0.2_spmd.sunk.clone | while | flops 33029636 | bytes 454753 | solution.py:95
  123.0 0.9 dynamic-slice_bitcast_fusion.3
  124.0 5.1 %fusion.56 = f32[512]{0:T(512)S(1)} fusion(f32[7,512]{1,0:T(8,128)S(1)} %get-tuple-element.98, f32[7,512]{1,0:T(8,128)S(1)} %get-tuple-element.99, f32[512]{0:T(512)S(1)} %bitcast.126, f32[7,512]{1,0:T(8,128)S(1)} %get-tuple-element.101, f32[7,512]{1,0:T(8,128)S(1)} %get-tuple-element.102, f32[512]{0:T(512)S(1)} %bitcast.125, ...), kind=kLoop, calls=%fused_computation.16.clone.1.clone | loop fusion | flops 33029632 | bytes 94208 | tf_op jit(solution)/shard_map/while/body/eval_jaxpr/reduce_sum | solution.py:29
  129.1 0.9 dynamic-slice_bitcast_fusion.3
  130.1 5.1 %fusion.56 = f32[512]{0:T(512)S(1)} fusion(f32[7,512]{1,0:T(8,128)S(1)} %get-tuple-element.98, f32[7,512]{1,0:T(8,128)S(1)} %get-tuple-element.99, f32[512]{0:T(512)S(1)} %bitcast.126, f32[7,512]{1,0:T(8,128)S(1)} %get-tuple-element.101, f32[7,512]{1,0:T(8,128)S(1)} %get-tuple-element.102, f32[512]{0:T(512)S(1)} %bitcast.125, ...), kind=kLoop, calls=%fused_computation.16.clone.1.clone | loop fusion | flops 33029632 | bytes 94208 | tf_op jit(solution)/shard_map/while/body/eval_jaxpr/reduce_sum | solution.py:29
  135.2 0.9 dynamic-slice_bitcast_fusion.3
  136.2 5.1 %fusion.56 = f32[512]{0:T(512)S(1)} fusion(f32[7,512]{1,0:T(8,128)S(1)} %get-tuple-element.98, f32[7,512]{1,0:T(8,128)S(1)} %get-tuple-element.99, f32[512]{0:T(512)S(1)} %bitcast.126, f32[7,512]{1,0:T(8,128)S(1)} %get-tuple-element.101, f32[7,512]{1,0:T(8,128)S(1)} %get-tuple-element.102, f32[512]{0:T(512)S(1)} %bitcast.125, ...), kind=kLoop, calls=%fused_computation.16.clone.1.clone | loop fusion | flops 33029632 | bytes 94208 | tf_op jit(solution)/shard_map/while/body/eval_jaxpr/reduce_sum | solution.py:29
  141.3 0.9 dynamic-slice_bitcast_fusion.3
  142.3 5.1 %fusion.56 = f32[512]{0:T(512)S(1)} fusion(f32[7,512]{1,0:T(8,128)S(1)} %get-tuple-element.98, f32[7,512]{1,0:T(8,128)S(1)} %get-tuple-element.99, f32[512]{0:T(512)S(1)} %bitcast.126, f32[7,512]{1,0:T(8,128)S(1)} %get-tuple-element.101, f32[7,512]{1,0:T(8,128)S(1)} %get-tuple-element.102, f32[512]{0:T(512)S(1)} %bitcast.125, ...), kind=kLoop, calls=%fused_computation.16.clone.1.clone | loop fusion | flops 33029632 | bytes 94208 | tf_op jit(solution)/shard_map/while/body/eval_jaxpr/reduce_sum | solution.py:29
  147.4 0.9 dynamic-slice_bitcast_fusion.3
  148.4 5.1 %fusion.56 = f32[512]{0:T(512)S(1)} fusion(f32[7,512]{1,0:T(8,128)S(1)} %get-tuple-element.98, f32[7,512]{1,0:T(8,128)S(1)} %get-tuple-element.99, f32[512]{0:T(512)S(1)} %bitcast.126, f32[7,512]{1,0:T(8,128)S(1)} %get-tuple-element.101, f32[7,512]{1,0:T(8,128)S(1)} %get-tuple-element.102, f32[512]{0:T(512)S(1)} %bitcast.125, ...), kind=kLoop, calls=%fused_computation.16.clone.1.clone | loop fusion | flops 33029632 | bytes 94208 | tf_op jit(solution)/shard_map/while/body/eval_jaxpr/reduce_sum | solution.py:29
  153.5 0.9 dynamic-slice_bitcast_fusion.3
  154.5 5.1 %fusion.56 = f32[512]{0:T(512)S(1)} fusion(f32[7,512]{1,0:T(8,128)S(1)} %get-tuple-element.98, f32[7,512]{1,0:T(8,128)S(1)} %get-tuple-element.99, f32[512]{0:T(512)S(1)} %bitcast.126, f32[7,512]{1,0:T(8,128)S(1)} %get-tuple-element.101, f32[7,512]{1,0:T(8,128)S(1)} %get-tuple-element.102, f32[512]{0:T(512)S(1)} %bitcast.125, ...), kind=kLoop, calls=%fused_computation.16.clone.1.clone | loop fusion | flops 33029632 | bytes 94208 | tf_op jit(solution)/shard_map/while/body/eval_jaxpr/reduce_sum | solution.py:29
  159.6 0.9 dynamic-slice_bitcast_fusion.3
  160.6 5.1 %fusion.56 = f32[512]{0:T(512)S(1)} fusion(f32[7,512]{1,0:T(8,128)S(1)} %get-tuple-element.98, f32[7,512]{1,0:T(8,128)S(1)} %get-tuple-element.99, f32[512]{0:T(512)S(1)} %bitcast.126, f32[7,512]{1,0:T(8,128)S(1)} %get-tuple-element.101, f32[7,512]{1,0:T(8,128)S(1)} %get-tuple-element.102, f32[512]{0:T(512)S(1)} %bitcast.125, ...), kind=kLoop, calls=%fused_computation.16.clone.1.clone | loop fusion | flops 33029632 | bytes 94208 | tf_op jit(solution)/shard_map/while/body/eval_jaxpr/reduce_sum | solution.py:29
  165.7 0.9 dynamic-slice_bitcast_fusion.3
  166.7 5.1 %fusion.56 = f32[512]{0:T(512)S(1)} fusion(f32[7,512]{1,0:T(8,128)S(1)} %get-tuple-element.98, f32[7,512]{1,0:T(8,128)S(1)} %get-tuple-element.99, f32[512]{0:T(512)S(1)} %bitcast.126, f32[7,512]{1,0:T(8,128)S(1)} %get-tuple-element.101, f32[7,512]{1,0:T(8,128)S(1)} %get-tuple-element.102, f32[512]{0:T(512)S(1)} %bitcast.125, ...), kind=kLoop, calls=%fused_computation.16.clone.1.clone | loop fusion | flops 33029632 | bytes 94208 | tf_op jit(solution)/shard_map/while/body/eval_jaxpr/reduce_sum | solution.py:29
  171.8 0.7 multiply_reduce_fusion
  172.5 0.4 convolution_bitcast_fusion.3
  172.9 45.8 %all-reduce = (f32[8]{0:T(128)S(1)}, f32[]{:T(128)}) all-reduce(f32[8]{0:T(128)S(1)} %convolution_bitcast_fusion.3, f32[]{:T(128)} %get-tuple-element.35), channel_id=1, replica_groups=mesh['role'=2,'dev'=16] {'role','dev'}, use_global_device_ids=true, to_apply=%region_3.4 | all-reduce | flops 9 | bytes 72 | tf_op jit(solution)/shard_map/psum | solution.py:116
  218.7 0.6 broadcast_multiply_fusion
  219.3 0.3 fusion.15
  220.9 0.6 fusion.23
  221.5 0.6 pad_maximum_fusion.1
  (84 shorter events, 1.0 us)
Async XLA Ops:
  0.6 4.6 %copy-start = (bf16[8,256,512]{2,1,0:T(8,128)(2,1)S(1)}, bf16[8,256,512]{2,1,0:T(8,128)(2,1)}, u32[]{:S(2)}) copy-start(bf16[8,256,512]{2,1,0:T(8,128)(2,1)} %param.28) | copy-start | bytes 6291460
  0.6 4.5 %copy-start.5 = (f32[8,512]{1,0:T(8,128)S(1)}, f32[8,512]{1,0:T(8,128)}, u32[]{:S(2)}) copy-start(f32[8,512]{1,0:T(8,128)} %param.19) | copy-start | bytes 49156
  0.7 4.5 %copy-start.9 = (s32[8]{0:T(128)S(1)}, s32[8]{0:T(128)}, u32[]{:S(2)}) copy-start(s32[8]{0:T(128)} %param.20) | copy-start | bytes 100
  0.7 19.6 %copy-start.8 = (s32[8,16]{1,0:T(8,128)S(1)}, s32[8,16]{1,0:T(8,128)}, u32[]{:S(2)}) copy-start(s32[8,16]{1,0:T(8,128)} %param.23) | copy-start | bytes 1540
  0.7 19.7 %copy-start.1 = (bf16[8,256,256]{2,1,0:T(8,128)(2,1)S(1)}, bf16[8,256,256]{2,1,0:T(8,128)(2,1)}, u32[]{:S(2)}) copy-start(bf16[8,256,256]{2,1,0:T(8,128)(2,1)} %param.29) | copy-start | bytes 3145732
  0.7 87.9 %copy-start.12 = (s32[1,16]{1,0:T(1,128)S(1)}, s32[1,16]{1,0:T(1,128)}, u32[]{:S(2)}) copy-start(s32[1,16]{1,0:T(1,128)} %param.25) | copy-start | bytes 196
  0.7 88.5 %copy-start.10 = (s32[1,16]{1,0:T(1,128)S(1)}, s32[1,16]{1,0:T(1,128)}, u32[]{:S(2)}) copy-start(s32[1,16]{1,0:T(1,128)} %param.26) | copy-start | bytes 196
  1.6 90.2 %copy-start.3 = (f32[8,3,512]{2,0,1:T(8,128)S(1)}, f32[8,3,512]{2,0,1:T(8,128)}, u32[]{:S(2)}) copy-start(f32[8,3,512]{2,0,1:T(8,128)} %param.17) | copy-start | bytes 147460
  1.6 90.3 %copy-start.6 = (s32[8,6]{1,0:T(8,128)S(1)}, s32[8,6]{1,0:T(8,128)}, u32[]{:S(2)}) copy-start(s32[8,6]{1,0:T(8,128)} %param.21) | copy-start | bytes 580
  1.6 90.5 %copy-start.11 = (s32[8]{0:T(128)S(1)}, s32[8]{0:T(128)}, u32[]{:S(2)}) copy-start(s32[8]{0:T(128)} %param.22) | copy-start | bytes 100
  1.6 90.6 %copy-start.4 = (f32[8,3,512]{2,0,1:T(8,128)S(1)}, f32[8,3,512]{2,0,1:T(8,128)}, u32[]{:S(2)}) copy-start(f32[8,3,512]{2,0,1:T(8,128)} %param.18) | copy-start | bytes 147460
  5.1 101.9 %copy-start.7 = (s32[8,16]{1,0:T(8,128)S(1)}, s32[8,16]{1,0:T(8,128)}, u32[]{:S(2)}) copy-start(s32[8,16]{1,0:T(8,128)} %param.24) | copy-start | bytes 1540
  5.9 86.4 %collective-permute-start.6 = (bf16[8,256]{1,0:T(8,128)(2,1)S(1)}, bf16[8,256]{1,0:T(8,128)(2,1)S(1)}, u32[]{:S(2)}, u32[]{:S(2)}) collective-permute-start(bf16[8,256]{1,0:T(8,128)(2,1)S(1)} %bitcast.130), channel_id=1, source_target_pairs={{0,3},{1,4},{2,5},{3,6},{4,7},{5,8},{6,9},{7,10},{8,11},{9,12},{10... | collective-permute-start | bytes 12296 | tf_op jit(solution)/shard_map/ppermute | solution.py:17
  11.7 81.9 %collective-permute-start.7 = (bf16[8,256]{1,0:T(8,128)(2,1)S(1)}, bf16[8,256]{1,0:T(8,128)(2,1)S(1)}, u32[]{:S(2)}, u32[]{:S(2)}) collective-permute-start(bf16[8,256]{1,0:T(8,128)(2,1)S(1)} %bitcast.131), channel_id=1, source_target_pairs={{0,2},{1,3},{2,4},{3,5},{4,6},{5,7},{6,8},{7,9},{8,10},{9,11},{10,... | collective-permute-start | bytes 12296 | tf_op jit(solution)/shard_map/ppermute | solution.py:17
  15.1 83.9 %collective-permute-start.8 = (bf16[8,256]{1,0:T(8,128)(2,1)S(1)}, bf16[8,256]{1,0:T(8,128)(2,1)S(1)}, u32[]{:S(2)}, u32[]{:S(2)}) collective-permute-start(bf16[8,256]{1,0:T(8,128)(2,1)S(1)} %bitcast.132), channel_id=1, source_target_pairs={{0,1},{1,2},{2,3},{3,4},{4,5},{5,6},{6,7},{7,8},{8,9},{9,10},{10,1... | collective-permute-start | bytes 12296 | tf_op jit(solution)/shard_map/ppermute | solution.py:17
  17.6 83.0 %collective-permute-start.9 = (bf16[8,256]{1,0:T(8,128)(2,1)S(1)}, bf16[8,256]{1,0:T(8,128)(2,1)S(1)}, u32[]{:S(2)}, u32[]{:S(2)}) collective-permute-start(bf16[8,256]{1,0:T(8,128)(2,1)S(1)} %bitcast.133), channel_id=1, source_target_pairs={{1,0},{2,1},{3,2},{4,3},{5,4},{6,5},{7,6},{8,7},{9,8},{10,9},{11,1... | collective-permute-start | bytes 12296 | tf_op jit(solution)/shard_map/ppermute | solution.py:17
  18.9 84.6 %collective-permute-start.10 = (bf16[8,256]{1,0:T(8,128)(2,1)S(1)}, bf16[8,256]{1,0:T(8,128)(2,1)S(1)}, u32[]{:S(2)}, u32[]{:S(2)}) collective-permute-start(bf16[8,256]{1,0:T(8,128)(2,1)S(1)} %bitcast.134), channel_id=1, source_target_pairs={{2,0},{3,1},{4,2},{5,3},{6,4},{7,5},{8,6},{9,7},{10,8},{11,9},{12,... | collective-permute-start | bytes 12296 | tf_op jit(solution)/shard_map/ppermute | solution.py:17
  92.3 12.6 %collective-permute-start.11 = (bf16[8,256]{1,0:T(8,128)(2,1)S(1)}, bf16[8,256]{1,0:T(8,128)(2,1)S(1)}, u32[]{:S(2)}, u32[]{:S(2)}) collective-permute-start(bf16[8,256]{1,0:T(8,128)(2,1)S(1)} %bitcast.135), channel_id=1, source_target_pairs={{3,0},{4,1},{5,2},{6,3},{7,4},{8,5},{9,6},{10,7},{11,8},{12,9},{13... | collective-permute-start | bytes 12296 | tf_op jit(solution)/shard_map/ppermute | solution.py:17
  93.6 16.1 %collective-permute-start = (f32[8,6,512]{2,1,0:T(8,128)S(1)}, f32[8,6,512]{2,1,0:T(8,128)S(1)}, u32[]{:S(2)}, u32[]{:S(2)}) collective-permute-start(f32[8,6,512]{2,1,0:T(8,128)S(1)} %pad_maximum_fusion), channel_id=1, source_target_pairs={{0,3},{1,4},{2,5},{3,6},{4,7},{5,8},{6,9},{7,10},{8,11},{9,12},{10... | collective-permute-start | bytes 294920 | tf_op jit(solution)/shard_map/ppermute | solution.py:17
  99.1 12.6 %collective-permute-start.1 = (f32[8,6,512]{2,1,0:T(8,128)S(1)}, f32[8,6,512]{2,1,0:T(8,128)S(1)}, u32[]{:S(2)}, u32[]{:S(2)}) collective-permute-start(f32[8,6,512]{2,1,0:T(8,128)S(1)} %pad_maximum_fusion), channel_id=1, source_target_pairs={{0,2},{1,3},{2,4},{3,5},{4,6},{5,7},{6,8},{7,9},{8,10},{9,11},{10,... | collective-permute-start | bytes 294920 | tf_op jit(solution)/shard_map/ppermute | solution.py:17
  100.7 11.7 %collective-permute-start.2 = (f32[8,6,512]{2,1,0:T(8,128)S(1)}, f32[8,6,512]{2,1,0:T(8,128)S(1)}, u32[]{:S(2)}, u32[]{:S(2)}) collective-permute-start(f32[8,6,512]{2,1,0:T(8,128)S(1)} %pad_maximum_fusion), channel_id=1, source_target_pairs={{0,1},{1,2},{2,3},{3,4},{4,5},{5,6},{6,7},{7,8},{8,9},{9,10},{10,1... | collective-permute-start | bytes 294920 | tf_op jit(solution)/shard_map/ppermute | solution.py:17
  103.5 10.1 %collective-permute-start.3 = (f32[8,6,512]{2,1,0:T(8,128)S(1)}, f32[8,6,512]{2,1,0:T(8,128)S(1)}, u32[]{:S(2)}, u32[]{:S(2)}) collective-permute-start(f32[8,6,512]{2,1,0:T(8,128)S(1)} %pad_maximum_fusion), channel_id=1, source_target_pairs={{1,0},{2,1},{3,2},{4,3},{5,4},{6,5},{7,6},{8,7},{9,8},{10,9},{11,1... | collective-permute-start | bytes 294920 | tf_op jit(solution)/shard_map/ppermute | solution.py:17
  104.9 9.5 %collective-permute-start.4 = (f32[8,6,512]{2,1,0:T(8,128)S(1)}, f32[8,6,512]{2,1,0:T(8,128)S(1)}, u32[]{:S(2)}, u32[]{:S(2)}) collective-permute-start(f32[8,6,512]{2,1,0:T(8,128)S(1)} %pad_maximum_fusion), channel_id=1, source_target_pairs={{2,0},{3,1},{4,2},{5,3},{6,4},{7,5},{8,6},{9,7},{10,8},{11,9},{12,... | collective-permute-start | bytes 294920 | tf_op jit(solution)/shard_map/ppermute | solution.py:17
  109.7 9.6 %collective-permute-start.5 = (f32[8,6,512]{2,1,0:T(8,128)S(1)}, f32[8,6,512]{2,1,0:T(8,128)S(1)}, u32[]{:S(2)}, u32[]{:S(2)}) collective-permute-start(f32[8,6,512]{2,1,0:T(8,128)S(1)} %pad_maximum_fusion), channel_id=1, source_target_pairs={{3,0},{4,1},{5,2},{6,3},{7,4},{8,5},{9,6},{10,7},{11,8},{12,9},{13... | collective-permute-start | bytes 294920 | tf_op jit(solution)/shard_map/ppermute | solution.py:17
  123.0 49.5 %copy-start.2 = (f32[8,8,512]{2,1,0:T(8,128)S(1)}, f32[8,8,512]{2,1,0:T(8,128)}, u32[]{:S(2)}) copy-start(f32[8,8,512]{2,1,0:T(8,128)} %param.31) | copy-start | bytes 393220
where the time goes:
time: 224 us; the launch traced here: 222 us
  blocking collectives  114 us (51%)
  other arithmetic  45.4 us (20%)
  starting transfers between devices  29.4 us (13%)
  local copies, waits for them, and re-layouts  16.4 us (7%)
  matrix products  10.4 us (5%)
  waiting for transfers between devices  4.28 us (2%)
  between operations  2.42 us (1%)
    all_gather x1, blocking collectives, shards(): lax.all_gather(group_moments, ('role', 'dev'), axis=0, tiled=True)  67.9 us
    psum x1, blocking collectives, shards(): lax.psum((projected, jnp.sum(image * image)), ('role', 'dev'))  45.8 us
    reduce_sum x8, other arithmetic, near_cluster(): return jnp.sum(projected * inverse * inverse * inverse, axis=(0, 2))  40.6 us
    ppermute x12, starting transfers between devices, passed_along(): return lax.ppermute(block, axis, route)  29.4 us
    squeeze x8, local copies, waits for them, and re-layouts, shards(): near_field = lax.map(near_cluster, (positions, gathered))  7.26 us
  transfers between devices with their start and end apart: 12, of which 1 were waited for; matrix products, arithmetic and copies ran while one was open for 5% of the time, Pallas kernels for 0%

commit v1 on v0

v1 whole, which is shorter than its diff:
```python
import functools

import jax
import jax.numpy as jnp
from jax import lax
from jax.experimental import pallas as pl
from jax.experimental.pallas import tpu as pltpu
from jax.sharding import PartitionSpec as P

RADIUS = 3
SIDES = 2 * RADIUS + 1
SOFTEN = 0.01
EPSILON = 1e-06
JB = 256
MESH = pl.DeviceIdType.MESH
NT = (((1,), (1,)), ((), ()))
NN = (((1,), (0,)), ((), ()))
TN = (((0,), (0,)), ((), ()))
F32 = jnp.float32
BF16 = jnp.bfloat16
AXES = ("role", "dev")


def mm(a, b, dims):
    return lax.dot_general(a, b, dims, preferred_element_type=F32)


def row_is(shape, k):
    return lax.broadcasted_iota(jnp.int32, shape, 0) == k


def place(roles, devs):
    me = lax.axis_index("role") * devs + lax.axis_index("dev")
    return me, roles * devs


def coords(linear, devs):
    return (linear // devs, lax.rem(linear, devs))


def greet(me, total, devs):
    barrier = pltpu.get_barrier_semaphore()

    def body(i, carry):
        pl.semaphore_signal(
            barrier,
            inc=1,
            device_id=coords(lax.rem(me + i, total), devs),
            device_id_type=MESH,
        )
        return carry

    lax.fori_loop(1, total, body, 0)
    return barrier


def live_mask(cnt_ref, shape):
    rows = lax.broadcasted_iota(jnp.int32, shape, 0)
    limit = jnp.zeros(shape, jnp.int32)
    for c in range(shape[0]):
        limit = jnp.where(rows == c, cnt_ref[c], limit)
    return lax.broadcasted_iota(jnp.int32, shape, 1) < limit


def halves(x):
    hi = x.astype(BF16).astype(F32)
    return jnp.concatenate([hi, x - hi], axis=0).astype(BF16)


def source_kernel(
    roles,
    devs,
    cnt,
    pos,
    nrm,
    area,
    kry,
    binv,
    maps,
    ups,
    paw,
    cntw,
    densw,
    momw,
    gmall,
    binv_v,
    maps_v,
    ups_v,
    local_sem,
    big_sem,
    send_sem,
    recv_sem,
    gsend,
    grecv,
):
    me, total = place(roles, devs)
    local, panels = area.shape
    coeffs = maps_v.shape[1]
    copies = []
    for c in range(local):
        copies.append(pltpu.make_async_copy(binv.at[c], binv_v.at[c], big_sem.at[c]))
    map_copy = pltpu.make_async_copy(maps, maps_v, local_sem.at[0])
    up_copy = pltpu.make_async_copy(ups, ups_v, local_sem.at[1])
    for copy in copies:
        copy.start()
    map_copy.start()
    up_copy.start()
    barrier = greet(me, total, devs)
    for c in range(local):
        paw[RADIUS, c, 0:3, :] = pos[c]
        paw[RADIUS, c, 3:6, :] = nrm[c] * area[c : c + 1, :]
    lane = lax.broadcasted_iota(jnp.int32, (1, 128), 1)
    counts = jnp.zeros((1, 128), jnp.int32)
    for c in range(local):
        counts = jnp.where(lane == c, cnt[c], counts)
    cntw[RADIUS] = counts
    pl.semaphore_wait(barrier, total - 1)

    def to_neighbours(ref, kind):
        made = []
        for n, d in enumerate([1, -1, 2, -2, 3, -3]):
            made.append(
                pltpu.make_async_remote_copy(
                    src_ref=ref.at[RADIUS],
                    dst_ref=ref.at[RADIUS - d],
                    send_sem=send_sem.at[kind, n],
                    recv_sem=recv_sem.at[kind, n],
                    device_id=coords(lax.rem(me + d + total, total), devs),
                    device_id_type=MESH,
                )
            )
        for copy in made:
            copy.start()
        return made

    sent = to_neighbours(paw, 0) + to_neighbours(cntw, 1)
    live = live_mask(cnt, (local, panels))
    current = kry[...].astype(BF16)
    density = jnp.zeros((local, panels), F32)
    for c in range(local):
        copies[c].wait()
        found = mm(current, binv_v[c], NT)
        density = jnp.where(row_is(found.shape, c), found, density)
    rounded = jnp.where(live, density, 0.0).astype(BF16)
    densw[RADIUS] = rounded.astype(F32)
    sent += to_neighbours(densw, 2)
    map_copy.wait()
    moments = jnp.zeros((local, coeffs), F32)
    for c in range(local):
        found = mm(rounded, maps_v[c], NT)
        moments = jnp.where(row_is(found.shape, c), found, moments)
    moments = moments.astype(BF16)
    momw[RADIUS] = moments.astype(F32)
    sent += to_neighbours(momw, 3)
    up_copy.wait()
    merged = jnp.zeros((local, coeffs), F32)
    for k in range(local):
        found = mm(moments, ups_v[k], NT)
        merged = jnp.where(row_is(found.shape, k), found, merged)
    gmall[me] = jnp.sum(merged, axis=0, keepdims=True)

    def group_copy(i):
        return pltpu.make_async_remote_copy(
            src_ref=gmall.at[me],
            dst_ref=gmall.at[me],
            send_sem=gsend.at[i],
            recv_sem=grecv.at[i],
            device_id=coords(lax.rem(me + i, total), devs),
            device_id_type=MESH,
        )

    def start_one(i, carry):
        group_copy(i).start()
        return carry

    def wait_one(i, carry):
        source = lax.rem(me - i + total, total)
        pltpu.make_async_remote_copy(
            src_ref=gmall.at[me],
            dst_ref=gmall.at[source],
            send_sem=gsend.at[i],
            recv_sem=grecv.at[i],
            device_id=coords(lax.rem(me + i, total), devs),
            device_id_type=MESH,
        ).wait()
        return carry

    lax.fori_loop(1, total, start_one, 0)
    for copy in sent:
        copy.wait()
    lax.fori_loop(1, total, wait_one, 0)


def splits(x):
    hi = x.astype(BF16).astype(F32)
    rest = x - hi
    mid = rest.astype(BF16).astype(F32)
    return hi, mid, rest - mid


def near_kernel(
    first, near, used, cntw, paw, densw, out, src_sq, src_pr, feat, sq0, pr0, sq1, pr1, acc
):
    local, panels = out.shape
    chunks = panels // 128
    one = jnp.ones((1, panels), F32)
    feat[...] = jnp.zeros(feat.shape, F32)

    def cluster_body(c, carry):
        x = paw[RADIUS, c, 0:3, :]
        feat[0:3, :] = x
        feat[3:4, :] = one
        feat[4:5, :] = jnp.sum(x * x, axis=0, keepdims=True)
        hi, mid, low = splits(feat[...])
        target = jnp.concatenate([hi, mid, hi, low, hi, mid], axis=0).astype(BF16)

        def slot_body(s, offset):
            listed = near[c, jnp.maximum(s - 1, 0)] - first[0]
            w = jnp.where(s == 0, RADIUS * local + c, listed)
            side = w // local
            inner = lax.rem(w, local)
            pa = paw[side, inner]
            y = pa[0:3]
            weighted = pa[3:6] * densw[side, pl.ds(inner, 1), :]
            feat[0:3, :] = -2.0 * y
            feat[3:4, :] = jnp.sum(y * y, axis=0, keepdims=True) + SOFTEN
            feat[4:5, :] = one
            hi, mid, low = splits(feat[...])
            sq = jnp.concatenate([hi, hi, mid, hi, low, mid], axis=0).astype(BF16)
            feat[0:3, :] = weighted
            feat[3:4, :] = -jnp.sum(y * weighted, axis=0, keepdims=True)
            feat[4:5, :] = jnp.zeros_like(one)
            hi, mid, low = splits(feat[...])
            pr = jnp.concatenate([hi, hi, mid, hi, low, mid], axis=0).astype(BF16)
            count = (cntw[side, 0, inner] + 127) // 128
            for b in range(chunks):
                src_sq[offset + b] = sq[:, b * 128 : (b + 1) * 128]
                src_pr[offset + b] = pr[:, b * 128 : (b + 1) * 128]
            return offset + count

        end = lax.fori_loop(0, used[c] + 1, slot_body, 0)
        rows = lax.broadcasted_iota(jnp.int32, (48, 128), 0)
        for b in range(3):
            src_sq[end + b] = jnp.where(rows == 3, 1.0, 0.0).astype(BF16)
            src_pr[end + b] = jnp.zeros((48, 128), BF16)

        def products(block, sq_ref, pr_ref):
            for half in range(2):
                part = pl.ds(half * 128, 128)
                sq_ref[part, :] = mm(src_sq[2 * block + half], target, TN)
                pr_ref[part, :] = mm(src_pr[2 * block + half], target, TN)

        def consume(sq_ref, pr_ref):
            for r in range(0, panels, 256):
                total = acc[:, r : r + 256]
                for j in range(0, JB, 8):
                    inverse = lax.rsqrt(sq_ref[j : j + 8, r : r + 256])
                    total = total + pr_ref[j : j + 8, r : r + 256] * inverse * (
                        inverse * inverse
                    )
                acc[:, r : r + 256] = total

        acc[...] = jnp.zeros(acc.shape, F32)
        blocks = (end + 1) // 2
        products(0, sq0, pr0)

        def pair_body(t, carry):
            products(2 * t + 1, sq1, pr1)
            consume(sq0, pr0)
            products(2 * t + 2, sq0, pr0)
            consume(sq1, pr1)
            return carry

        lax.fori_loop(0, blocks // 2, pair_body, 0)

        @pl.when(lax.rem(blocks, 2) == 1)
        def _():
            consume(sq0, pr0)

        out[pl.ds(c, 1), :] = jnp.sum(acc[...], axis=0, keepdims=True)
        return carry

    lax.fori_loop(0, local, cluster_body, 0)


def finish_kernel(
    roles,
    devs,
    cnt,
    glist,
    gkind,
    llist,
    lkind,
    momw,
    gmall,
    near,
    densw,
    kry,
    maps,
    ups,
    fars,
    nxt,
    hess,
    maps_v,
    ups_v,
    fars_v,
    red,
    local_sem,
    send_sem,
    recv_sem,
):
    me, total = place(roles, devs)
    local, panels = near.shape
    coeffs = maps_v.shape[1]
    kinds = fars_v.shape[1]
    window = SIDES * local
    far_copies = [
        pltpu.make_async_copy(fars.at[level], fars_v.at[level], local_sem.at[level])
        for level in range(2)
    ]
    up_copy = pltpu.make_async_copy(ups, ups_v, local_sem.at[2])
    map_copy = pltpu.make_async_copy(maps, maps_v, local_sem.at[3])
    far_copies[1].start()
    far_copies[0].start()
    up_copy.start()
    map_copy.start()
    barrier = greet(me, total, devs)

    groups = gmall[...].reshape(total, coeffs)
    g_rows = lax.broadcasted_iota(jnp.int32, (kinds, total), 0)
    g_lanes = lax.broadcasted_iota(jnp.int32, (kinds, total), 1)
    g_hot = jnp.zeros((kinds, total), F32)
    for n in range(glist.shape[1]):
        g_hot += jnp.where((g_rows == gkind[0, n]) & (g_lanes == glist[0, n]), 1.0, 0.0)
    g_hot = g_hot.astype(BF16)
    hi, mid, low = splits(groups)
    g_sum = mm(g_hot, hi.astype(BF16), NN) + mm(g_hot, mid.astype(BF16), NN)
    g_sum += mm(g_hot, low.astype(BF16), NN)
    g_both = halves(g_sum)

    lanes = lax.broadcasted_iota(jnp.int32, (local, window), 1)
    base = (me - RADIUS) * local
    hots = [jnp.zeros((local, window), F32) for _ in range(kinds)]
    for n in range(llist.shape[1]):
        hit = lanes == (llist[:, n : n + 1] - base)
        kind = jnp.broadcast_to(lkind[:, n : n + 1], (local, window))
        for o in range(kinds):
            hots[o] = hots[o] + jnp.where(hit & (kind == o), 1.0, 0.0)
    hot = jnp.concatenate(hots, axis=0).astype(BF16)
    summed = mm(hot, momw[...].reshape(window, coeffs).astype(BF16), NN)

    far_copies[1].wait()
    g_parts = jnp.zeros((kinds, coeffs), F32)
    for o in range(kinds):
        found = mm(g_both, fars_v[1, o], NT)
        found = found[:kinds] + found[kinds:]
        g_parts = jnp.where(row_is(found.shape, o), found, g_parts)
    g_local = jnp.sum(g_parts, axis=0, keepdims=True).astype(BF16)
    far_copies[0].wait()
    leaf = jnp.zeros((local, coeffs), F32)
    for o in range(kinds):
        found = mm(halves(summed[o * local : (o + 1) * local]), fars_v[0, o], NT)
        leaf = leaf + found[:local] + found[local:]
    up_copy.wait()
    g_wide = jnp.broadcast_to(g_local.astype(F32), (local, coeffs)).astype(BF16)
    down = jnp.zeros((local, coeffs), F32)
    for k in range(local):
        found = mm(g_wide, ups_v[k], NN)
        down = jnp.where(row_is(found.shape, k), found, down)
    leaf = (leaf + down).astype(BF16)
    map_copy.wait()
    far = jnp.zeros((local, panels), F32)
    for c in range(local):
        found = mm(leaf, maps_v[c], NN)
        far = jnp.where(row_is(found.shape, c), found, far)
    live = live_mask(cnt, (local, panels))
    image = jnp.where(live, 0.5 * densw[RADIUS] + near[...] + far, 0.0)

    lane = lax.broadcasted_iota(jnp.int32, (1, 128), 1)
    count = kry.shape[0]
    row = jnp.zeros((1, 128), F32)
    for k in range(count + 1):
        part = image * (kry[k] if k < count else image)
        value = jnp.sum(jnp.sum(part, axis=0, keepdims=True), axis=1, keepdims=True)
        row = jnp.where(lane == k, value, row)
    red[me] = row
    pl.semaphore_wait(barrier, total - 1)

    def one(i):
        source = lax.rem(me - i + total, total)
        target = coords(lax.rem(me + i, total), devs)

        def copy(dst):
            return pltpu.make_async_remote_copy(
                src_ref=red.at[me],
                dst_ref=red.at[dst],
                send_sem=send_sem.at[i],
                recv_sem=recv_sem.at[i],
                device_id=target,
                device_id_type=MESH,
            )

        return copy, source

    def start_one(i, carry):
        one(i)[0](me).start()
        return carry

    def wait_one(i, carry):
        copy, source = one(i)
        copy(source).wait()
        return carry

    lax.fori_loop(1, total, start_one, 0)
    lax.fori_loop(1, total, wait_one, 0)
    scale = 1.0 / (total * local * panels)
    sums = jnp.sum(red[...], axis=0) * scale
    rest = image
    energy = sums[:, count : count + 1]
    for k in range(count):
        c_k = sums[:, k : k + 1]
        rest = rest - c_k * kry[k]
        energy = energy - c_k * c_k
    height = jnp.sqrt(energy + EPSILON)
    nxt[...] = rest / height
    hess[...] = jnp.where(lane == count, height, sums)


def shards(
    roles,
    devs,
    positions,
    normals,
    panel_areas,
    panel_counts,
    near_lists,
    near_counts,
    leaf_lists,
    leaf_kinds,
    group_lists,
    group_kinds,
    block_inverse,
    moment_maps,
    up_operators,
    far_operators,
    krylov_basis,
):
    local, _, panels = positions.shape
    coeffs = moment_maps.shape[1]
    total = roles * devs
    vmem = pl.BlockSpec(memory_space=pltpu.VMEM)
    smem = pl.BlockSpec(memory_space=pltpu.SMEM)
    hbm = pl.BlockSpec(memory_space=pl.ANY)
    dma = pltpu.SemaphoreType.DMA
    paw, cntw, densw, momw, gmall = pl.pallas_call(
        functools.partial(source_kernel, roles, devs),
        name="sources",
        out_shape=(
            jax.ShapeDtypeStruct((SIDES, local, 6, panels), F32),
            jax.ShapeDtypeStruct((SIDES, 1, 128), jnp.int32),
            jax.ShapeDtypeStruct((SIDES, local, panels), F32),
            jax.ShapeDtypeStruct((SIDES, local, coeffs), F32),
            jax.ShapeDtypeStruct((total, 1, coeffs), F32),
        ),
        in_specs=[smem, vmem, vmem, vmem, vmem, hbm, hbm, hbm],
        out_specs=(vmem,) * 5,
        scratch_shapes=[
            pltpu.VMEM(block_inverse.shape, BF16),
            pltpu.VMEM(moment_maps.shape, BF16),
            pltpu.VMEM(up_operators.shape, BF16),
            dma((2,)),
            dma((local,)),
            dma((4, 6)),
            dma((4, 6)),
            dma((total,)),
            dma((total,)),
        ],
        compiler_params=pltpu.CompilerParams(
            collective_id=0, has_side_effects=True, vmem_limit_bytes=20 << 20
        ),
    )(
        panel_counts,
        positions,
        normals,
        panel_areas,
        krylov_basis[-1],
        block_inverse,
        moment_maps,
        up_operators,
    )
    own = lax.axis_index(AXES)
    first = jnp.reshape((own - RADIUS) * local, (1,)).astype(jnp.int32)
    room = (near_lists.shape[1] + 1) * (panels // 128) + 8
    near = pl.pallas_call(
        near_kernel,
        name="near",
        out_shape=jax.ShapeDtypeStruct((local, panels), F32),
        in_specs=[smem, smem, smem, smem, vmem, vmem],
        out_specs=vmem,
        scratch_shapes=[
            pltpu.VMEM((room, 48, 128), BF16),
            pltpu.VMEM((room, 48, 128), BF16),
            pltpu.VMEM((8, panels), F32),
            pltpu.VMEM((JB, panels), F32),
            pltpu.VMEM((JB, panels), F32),
            pltpu.VMEM((JB, panels), F32),
            pltpu.VMEM((JB, panels), F32),
            pltpu.VMEM((8, panels), F32),
        ],
        compiler_params=pltpu.CompilerParams(vmem_limit_bytes=20 << 20),
    )(first, near_lists, near_counts, cntw, paw, densw)
    nxt, hess = pl.pallas_call(
        functools.partial(finish_kernel, roles, devs),
        name="finish",
        out_shape=(
            jax.ShapeDtypeStruct((local, panels), F32),
            jax.ShapeDtypeStruct((1, 128), F32),
        ),
        in_specs=[smem, smem, smem] + [vmem] * 7 + [hbm] * 3,
        out_specs=(vmem, vmem),
        scratch_shapes=[
            pltpu.VMEM(moment_maps.shape, BF16),
            pltpu.VMEM(up_operators.shape, BF16),
            pltpu.VMEM(far_operators.shape, BF16),
            pltpu.VMEM((total, 1, 128), F32),
            dma((4,)),
            dma((total,)),
            dma((total,)),
        ],
        compiler_params=pltpu.CompilerParams(
            collective_id=1, has_side_effects=True, vmem_limit_bytes=20 << 20
        ),
    )(
        panel_counts,
        group_lists,
        group_kinds,
        leaf_lists,
        leaf_kinds,
        momw,
        gmall,
        near,
        densw,
        krylov_basis,
        moment_maps,
        up_operators,
        far_operators,
    )
    return nxt, hess[0, : krylov_basis.shape[0] + 1]


def solution(mesh):
    roles, devs = mesh.shape["role"], mesh.shape["dev"]
    return jax.shard_map(
        functools.partial(shards, roles, devs),
        mesh=mesh,
        in_specs=(
            P(AXES, None, None),
            P(AXES, None, None),
            P(AXES, None),
            P(AXES),
            P(AXES, None),
            P(AXES),
            P(AXES, None),
            P(AXES, None),
            P(AXES, None),
            P(AXES, None),
            P(AXES, None, None),
            P(AXES, None, None),
            P(),
            P(),
            P(None, AXES, None),
        ),
        out_specs=(P(AXES, None), P()),
        check_vma=False,
    )
```

time: 224 us -> 70.7 us (0.32)
  blocking collectives: 114 us -> 0 us
  Pallas kernels: 0 us -> 54.9 us
  other arithmetic: 45.4 us -> 0 us
  starting transfers between devices: 29.4 us -> 0 us
  matrix products: 10.4 us -> 0 us
  waiting for transfers between devices: 4.28 us -> 0 us
  local copies, waits for them, and re-layouts: 16.4 us -> 13.6 us
    all_gather x1 -> x0, blocking collectives: 67.9 us -> none  [shards(): lax.all_gather(group_moments, ('role', 'dev'), axis=0, tiled=True)]
    pallas_call x0 -> x3, Pallas kernels: none -> 54.9 us  [the longest x1 24.8 us: shards(): pl.pallas_call(functools.partial(source_kernel, roles, devs), name='sourc...]
    psum x1 -> x0, blocking collectives: 45.8 us -> none  [shards(): lax.psum((projected, jnp.sum(image * image)), ('role', 'dev'))]
    reduce_sum x9 -> x0, other arithmetic: 41.3 us -> none  [the longest x8 40.6 us: near_cluster(): return jnp.sum(projected * inverse * inverse * inverse, axis=(0, 2))]
    ppermute x12 -> x0, starting transfers between devices: 29.4 us -> none  [passed_along(): return lax.ppermute(block, axis, route)]
    dot_general x11 -> x0, matrix products: 10.4 us -> none  [the longest x2 4.27 us: translate(): return jnp.einsum('goc,oqc->gq', summed, operators, precision=HIGH)]
    unnamed x39, local copies, waits for them, and re-layouts: 3.46 us -> 12.4 us
    squeeze x8 -> x2, local copies, waits for them, and re-layouts: 7.26 us -> 1.24 us  [the longest x1 0.72 us: shards(): krylov_basis[-1]]
  transfers between devices with their start and end apart: 12 -> 0, of which waited for: 1 -> 0; matrix products, arithmetic and copies ran while one was open for 5% -> 0% of each run, Pallas kernels for 0% -> 0%
where the time goes in v1:
time: 70.7 us; the launch traced here: 69.3 us
  Pallas kernels  54.9 us (78%)
  local copies, waits for them, and re-layouts  13.6 us (19%)
  between operations  0.79 us (1%)
    pallas_call x1, Pallas kernels, shards(): pl.pallas_call(functools.partial(source_kernel, roles, devs), name='sourc...  24.8 us
    pallas_call x1, Pallas kernels, shards(): pl.pallas_call(near_kernel, name='near', out_shape=jax.ShapeDtypeStruct((...  19.2 us
    unnamed x39, local copies, waits for them, and re-layouts  12.4 us
    pallas_call x1, Pallas kernels, shards(): pl.pallas_call(functools.partial(finish_kernel, roles, devs), name='finis...  10.9 us

profile of v1, /device:TPU:0, one launch (start us, length us, event | category | flops | bytes accessed | tf_op | source)
XLA Modules:
  0.0 69.3 jit_solution(6294897693220973736)
XLA Ops:
  0.6 0.8 %copy.17.pos = f32[8,3,512]{2,1,0:T(4,128)S(1)} copy(f32[8,3,512]{2,0,1:T(8,128)} %param.15) | data formatting | bytes 98304 | tf_op args[0]
  1.5 0.8 %copy.18.nrm = f32[8,3,512]{2,1,0:T(4,128)S(1)} copy(f32[8,3,512]{2,0,1:T(8,128)} %param.16) | data formatting | bytes 98304 | tf_op args[1]
  2.3 0.7 %slice_bitcast_fusion.kry = f32[8,512]{1,0:T(8,128)S(1)} fusion(f32[8,8,512]{2,1,0:T(8,128)} %kry.1), kind=kLoop, calls=%fused_computation | loop fusion | bytes 32768 | tf_op jit(solution)/shard_map/squeeze | solution.py:486
  3.0 0.0 copy-start
  3.0 1.6 %copy-done = bf16[8,256,512]{2,1,0:T(8,128)(2,1)S(1)} copy-done((bf16[8,256,512]{2,1,0:T(8,128)(2,1)S(1)}, bf16[8,256,512]{2,1,0:T(8,128)(2,1)}, u32[]{:S(2)}) %copy-start) | copy-done | bytes 2097176
  4.6 0.0 copy-start.2
  4.6 2.2 %copy-done.2 = bf16[8,512,512]{2,1,0:T(8,128)(2,1)S(1)} copy-done((bf16[8,512,512]{2,1,0:T(8,128)(2,1)S(1)}, bf16[8,512,512]{2,1,0:T(8,128)(2,1)}, u32[]{:S(2)}) %copy-start.2) | copy-done | bytes 4194328
  6.8 0.0 copy-start.3
  6.8 1.2 %copy-done.3 = bf16[8,256,256]{2,1,0:T(8,128)(2,1)S(1)} copy-done((bf16[8,256,256]{2,1,0:T(8,128)(2,1)S(1)}, bf16[8,256,256]{2,1,0:T(8,128)(2,1)}, u32[]{:S(2)}) %copy-start.3) | copy-done | bytes 1048600
  8.0 0.0 copy-start.9
  8.0 0.7 %copy-done.9 = f32[8,512]{1,0:T(8,128)S(1)} copy-done((f32[8,512]{1,0:T(8,128)S(1)}, f32[8,512]{1,0:T(8,128)}, u32[]{:S(2)}) %copy-start.9) | copy-done | bytes 16408
  8.8 0.0 copy-start.13
  8.8 0.7 copy-done.13
  9.4 0.0 copy-start.10
  9.4 0.0 copy-start.15
  9.4 0.0 copy-start.1
  9.4 0.0 copy-start.4
  9.4 0.0 copy-start.8
  9.4 0.0 copy-start.11
  9.4 0.0 copy-start.12
  9.5 0.0 copy-start.14
  9.5 0.0 copy-start.16
  9.5 0.0 copy-start.17
  9.5 24.8 %sources.1 = (f32[7,8,6,512]{3,2,1,0:T(8,128)S(1)}, s32[7,1,128]{2,1,0:T(1,128)S(1)}, f32[7,8,512]{2,1,0:T(8,128)S(1)}, f32[7,8,256]{2,1,0:T(8,128)S(1)}, f32[32,1,256]{2,1,0:T(1,128)S(1)}) custom-call(s32[8]{0:T(128)S(1)} %copy-done.13, f32[8,3,512]{2,1,0:T(4,128)S(1)} %copy.17.pos, f32[8,3,512]{2,1,0:T(4,128)S(1)} %copy.18.nrm, f32[8,512]{1,0:T(8,128)S(1)} %copy-done.9, ...), custom_call_target="tpu_custom_call" | custom-call | tf_op jit(solution)/shard_map/sources/pallas_call | solution.py:455
  34.3 0.0 copy-start.6
  34.3 0.9 %copy-done.6 = f32[7,8,6,512]{3,2,1,0:T(8,128)} copy-done((f32[7,8,6,512]{3,2,1,0:T(8,128)}, f32[7,8,6,512]{3,2,1,0:T(8,128)S(1)}, u32[]{:S(2)}) %copy-start.6) | copy-done | bytes 688152
  35.2 0.0 copy-done.10
  35.2 0.0 copy-done.15
  35.2 0.0 copy-start.7
  35.2 1.2 %copy-done.7 = f32[7,8,6,512]{3,2,1,0:T(8,128)S(1)} copy-done((f32[7,8,6,512]{3,2,1,0:T(8,128)S(1)}, f32[7,8,6,512]{3,2,1,0:T(8,128)}, u32[]{:S(2)}) %copy-start.7) | copy-done | bytes 688152
  36.4 19.2 %near.2 = f32[8,512]{1,0:T(8,128)S(1)} custom-call(s32[1]{0:T(128)} %bitcast.1.first, s32[8,6]{1,0:T(8,128)S(1)} %copy-done.10, s32[8]{0:T(128)S(1)} %copy-done.15, s32[7,1,128]{2,1,0:T(1,128)S(1)} %get-tuple-element.11.cntw, f32[7,8,6,512]{3,2,1,0:T(8,128)S(1)} %copy-done.7, f32[7,8,512]{2,1,0:T(8,128)S(1)} %get-tuple-element.13.densw), custom_call_target="tpu_custom_call" | custom-call | tf_op jit(solution)/shard_map/near/pallas_call | solution.py:494
  55.6 0.0 copy-done.1
  55.6 0.0 copy-done.4
  55.6 0.0 copy-done.8
  55.6 0.0 copy-done.11
  55.6 0.0 copy-done.12
  55.6 0.0 copy-done.14
  55.7 0.0 copy-done.16
  55.7 0.0 copy-done.17
  55.7 0.0 copy-start.5
  55.7 1.6 %copy-done.5 = bf16[2,8,256,256]{3,2,1,0:T(8,128)(2,1)S(1)} copy-done((bf16[2,8,256,256]{3,2,1,0:T(8,128)(2,1)S(1)}, bf16[2,8,256,256]{3,2,1,0:T(8,128)(2,1)}, u32[]{:S(2)}) %copy-start.5) | copy-done | bytes 2097176
  57.3 10.9 %finish.1 = (f32[8,512]{1,0:T(8,128)S(1)}, f32[1,128]{1,0:T(1,128)S(1)}) custom-call(s32[8]{0:T(128)S(1)} %copy-done.14, s32[1,16]{1,0:T(1,128)S(1)} %copy-done.16, s32[1,16]{1,0:T(1,128)S(1)} %copy-done.17, s32[8,16]{1,0:T(8,128)S(1)} %copy-done.11, s32[8,16]{1,0:T(8,128)S(1)} %copy-done.12, f32[7,8,256]{2,1,0:T(8,128)S(1)} %get-tuple-element.9.momw, ...), custom_call_target="tpu_custom_call" | custom-call | tf_op jit(solution)/shard_map/finish/pallas_call | solution.py:512
  68.2 0.5 slice_bitcast_fusion.1
  68.7 0.6 copy.20
Async XLA Ops:
  3.0 1.6 %copy-start = (bf16[8,256,512]{2,1,0:T(8,128)(2,1)S(1)}, bf16[8,256,512]{2,1,0:T(8,128)(2,1)}, u32[]{:S(2)}) copy-start(bf16[8,256,512]{2,1,0:T(8,128)(2,1)} %maps.3) | copy-start | bytes 6291460
  4.6 2.2 %copy-start.2 = (bf16[8,512,512]{2,1,0:T(8,128)(2,1)S(1)}, bf16[8,512,512]{2,1,0:T(8,128)(2,1)}, u32[]{:S(2)}) copy-start(bf16[8,512,512]{2,1,0:T(8,128)(2,1)} %binv.1) | copy-start | bytes 12582916
  6.8 1.2 %copy-start.3 = (bf16[8,256,256]{2,1,0:T(8,128)(2,1)S(1)}, bf16[8,256,256]{2,1,0:T(8,128)(2,1)}, u32[]{:S(2)}) copy-start(bf16[8,256,256]{2,1,0:T(8,128)(2,1)} %ups.3) | copy-start | bytes 3145732
  8.0 0.7 %copy-start.9 = (f32[8,512]{1,0:T(8,128)S(1)}, f32[8,512]{1,0:T(8,128)}, u32[]{:S(2)}) copy-start(f32[8,512]{1,0:T(8,128)} %area.1) | copy-start | bytes 49156
  8.8 0.7 copy-start.13
  9.4 25.8 %copy-start.10 = (s32[8,6]{1,0:T(8,128)S(1)}, s32[8,6]{1,0:T(8,128)}, u32[]{:S(2)}) copy-start(s32[8,6]{1,0:T(8,128)} %near.3) | copy-start | bytes 580
  9.4 25.8 %copy-start.15 = (s32[8]{0:T(128)S(1)}, s32[8]{0:T(128)}, u32[]{:S(2)}) copy-start(s32[8]{0:T(128)} %used.1) | copy-start | bytes 100
  9.4 46.2 %copy-start.1 = (bf16[8,256,512]{2,1,0:T(8,128)(2,1)S(1)}, bf16[8,256,512]{2,1,0:T(8,128)(2,1)}, u32[]{:S(2)}) copy-start(bf16[8,256,512]{2,1,0:T(8,128)(2,1)} %maps.3) | copy-start | bytes 6291460
  9.4 46.2 %copy-start.4 = (bf16[8,256,256]{2,1,0:T(8,128)(2,1)S(1)}, bf16[8,256,256]{2,1,0:T(8,128)(2,1)}, u32[]{:S(2)}) copy-start(bf16[8,256,256]{2,1,0:T(8,128)(2,1)} %ups.3) | copy-start | bytes 3145732
  9.4 46.2 %copy-start.8 = (f32[8,8,512]{2,1,0:T(8,128)S(1)}, f32[8,8,512]{2,1,0:T(8,128)}, u32[]{:S(2)}) copy-start(f32[8,8,512]{2,1,0:T(8,128)} %kry.1) | copy-start | bytes 393220
  9.4 46.2 %copy-start.11 = (s32[8,16]{1,0:T(8,128)S(1)}, s32[8,16]{1,0:T(8,128)}, u32[]{:S(2)}) copy-start(s32[8,16]{1,0:T(8,128)} %llist.1) | copy-start | bytes 1540
  9.4 46.2 %copy-start.12 = (s32[8,16]{1,0:T(8,128)S(1)}, s32[8,16]{1,0:T(8,128)}, u32[]{:S(2)}) copy-start(s32[8,16]{1,0:T(8,128)} %lkind.1) | copy-start | bytes 1540
  9.5 46.2 %copy-start.14 = (s32[8]{0:T(128)S(1)}, s32[8]{0:T(128)}, u32[]{:S(2)}) copy-start(s32[8]{0:T(128)} %cnt.3) | copy-start | bytes 100
  9.5 46.2 %copy-start.16 = (s32[1,16]{1,0:T(1,128)S(1)}, s32[1,16]{1,0:T(1,128)}, u32[]{:S(2)}) copy-start(s32[1,16]{1,0:T(1,128)} %glist.1) | copy-start | bytes 196
  9.5 46.2 %copy-start.17 = (s32[1,16]{1,0:T(1,128)S(1)}, s32[1,16]{1,0:T(1,128)}, u32[]{:S(2)}) copy-start(s32[1,16]{1,0:T(1,128)} %gkind.1) | copy-start | bytes 196
  34.3 0.9 %copy-start.6 = (f32[7,8,6,512]{3,2,1,0:T(8,128)}, f32[7,8,6,512]{3,2,1,0:T(8,128)S(1)}, u32[]{:S(2)}) copy-start(f32[7,8,6,512]{3,2,1,0:T(8,128)S(1)} %get-tuple-element.12.paw) | copy-start | bytes 2064388
  35.2 1.2 %copy-start.7 = (f32[7,8,6,512]{3,2,1,0:T(8,128)S(1)}, f32[7,8,6,512]{3,2,1,0:T(8,128)}, u32[]{:S(2)}) copy-start(f32[7,8,6,512]{3,2,1,0:T(8,128)} %copy-done.6) | copy-start | bytes 2064388
  55.7 1.6 %copy-start.5 = (bf16[2,8,256,256]{3,2,1,0:T(8,128)(2,1)S(1)}, bf16[2,8,256,256]{3,2,1,0:T(8,128)(2,1)}, u32[]{:S(2)}) copy-start(bf16[2,8,256,256]{3,2,1,0:T(8,128)(2,1)} %fars.1) | copy-start | bytes 6291460

commit v2 on v1

--- a/solution.py
+++ b/solution.py
@@ -78,11 +78,15 @@
     binv,
     maps,
     ups,
-    paw,
+    posw,
+    anw,
     cntw,
     densw,
     momw,
     gmall,
+    nrm_v,
+    area_v,
+    kry_v,
     binv_v,
     maps_v,
     ups_v,
@@ -101,14 +105,21 @@
         copies.append(pltpu.make_async_copy(binv.at[c], binv_v.at[c], big_sem.at[c]))
     map_copy = pltpu.make_async_copy(maps, maps_v, local_sem.at[0])
     up_copy = pltpu.make_async_copy(ups, ups_v, local_sem.at[1])
-    for copy in copies:
+    small = [
+        pltpu.make_async_copy(pos, posw.at[RADIUS], local_sem.at[2]),
+        pltpu.make_async_copy(nrm, nrm_v, local_sem.at[3]),
+        pltpu.make_async_copy(area, area_v, local_sem.at[4]),
+        pltpu.make_async_copy(kry.at[kry.shape[0] - 1], kry_v, local_sem.at[5]),
+    ]
+    for copy in small + copies:
         copy.start()
     map_copy.start()
     up_copy.start()
     barrier = greet(me, total, devs)
-    for c in range(local):
-        paw[RADIUS, c, 0:3, :] = pos[c]
-        paw[RADIUS, c, 3:6, :] = nrm[c] * area[c : c + 1, :]
+    for copy in small:
+        copy.wait()
+    parts = [nrm_v[a] * area_v[...] for a in range(3)]
+    anw[RADIUS] = jnp.concatenate(parts, axis=0).astype(BF16)
     lane = lax.broadcasted_iota(jnp.int32, (1, 128), 1)
     counts = jnp.zeros((1, 128), jnp.int32)
     for c in range(local):
@@ -133,16 +144,16 @@
             copy.start()
         return made
 
-    sent = to_neighbours(paw, 0) + to_neighbours(cntw, 1)
+    sent = to_neighbours(posw, 0) + to_neighbours(anw, 4) + to_neighbours(cntw, 1)
     live = live_mask(cnt, (local, panels))
-    current = kry[...].astype(BF16)
+    current = kry_v[...].astype(BF16)
     density = jnp.zeros((local, panels), F32)
     for c in range(local):
         copies[c].wait()
         found = mm(current, binv_v[c], NT)
         density = jnp.where(row_is(found.shape, c), found, density)
     rounded = jnp.where(live, density, 0.0).astype(BF16)
-    densw[RADIUS] = rounded.astype(F32)
+    densw[RADIUS] = rounded
     sent += to_neighbours(densw, 2)
     map_copy.wait()
     moments = jnp.zeros((local, coeffs), F32)
@@ -150,7 +161,7 @@
         found = mm(rounded, maps_v[c], NT)
         moments = jnp.where(row_is(found.shape, c), found, moments)
     moments = moments.astype(BF16)
-    momw[RADIUS] = moments.astype(F32)
+    momw[RADIUS] = moments
     sent += to_neighbours(momw, 3)
     up_copy.wait()
     merged = jnp.zeros((local, coeffs), F32)
@@ -199,39 +210,50 @@
 
 
 def near_kernel(
-    first, near, used, cntw, paw, densw, out, src_sq, src_pr, feat, sq0, pr0, sq1, pr1, acc
+    first, near, used, cntw, posw, anw, densw, out, src_sq, src_pr, weight, sq0, pr0, sq1, pr1, acc
 ):
     local, panels = out.shape
     chunks = panels // 128
-    one = jnp.ones((1, panels), F32)
-    feat[...] = jnp.zeros(feat.shape, F32)
+    shape = (8, panels)
+    rows = lax.broadcasted_iota(jnp.int32, shape, 0)
+    for side in range(SIDES):
+        dens = densw[side].astype(F32)
+        products_an = anw[side].astype(F32)
+        for a in range(3):
+            weight[side, a] = products_an[a * local : (a + 1) * local] * dens
+
+    def vectors(ref, side, inner):
+        return [
+            jnp.broadcast_to(ref[side, a, pl.ds(inner, 1), :], shape) for a in range(3)
+        ]
+
+    def stack(values):
+        feat = jnp.zeros(shape, F32)
+        for k, value in enumerate(values):
+            feat = jnp.where(rows == k, value, feat)
+        return feat
+
+    def pack(feat, order):
+        parts = splits(feat)
+        return jnp.concatenate([parts[k] for k in order], axis=0).astype(BF16)
 
     def cluster_body(c, carry):
-        x = paw[RADIUS, c, 0:3, :]
-        feat[0:3, :] = x
-        feat[3:4, :] = one
-        feat[4:5, :] = jnp.sum(x * x, axis=0, keepdims=True)
-        hi, mid, low = splits(feat[...])
-        target = jnp.concatenate([hi, mid, hi, low, hi, mid], axis=0).astype(BF16)
+        x0, x1, x2 = vectors(posw, RADIUS, c)
+        norm = x0 * x0 + x1 * x1 + x2 * x2
+        target = pack(stack([x0, x1, x2, 1.0, norm]), (0, 1, 0, 2, 0, 1))
 
         def slot_body(s, offset):
             listed = near[c, jnp.maximum(s - 1, 0)] - first[0]
             w = jnp.where(s == 0, RADIUS * local + c, listed)
             side = w // local
             inner = lax.rem(w, local)
-            pa = paw[side, inner]
-            y = pa[0:3]
-            weighted = pa[3:6] * densw[side, pl.ds(inner, 1), :]
-            feat[0:3, :] = -2.0 * y
-            feat[3:4, :] = jnp.sum(y * y, axis=0, keepdims=True) + SOFTEN
-            feat[4:5, :] = one
-            hi, mid, low = splits(feat[...])
-            sq = jnp.concatenate([hi, hi, mid, hi, low, mid], axis=0).astype(BF16)
-            feat[0:3, :] = weighted
-            feat[3:4, :] = -jnp.sum(y * weighted, axis=0, keepdims=True)
-            feat[4:5, :] = jnp.zeros_like(one)
-            hi, mid, low = splits(feat[...])
-            pr = jnp.concatenate([hi, hi, mid, hi, low, mid], axis=0).astype(BF16)
+            y0, y1, y2 = vectors(posw, side, inner)
+            w0, w1, w2 = vectors(weight, side, inner)
+            norm = y0 * y0 + y1 * y1 + y2 * y2 + SOFTEN
+            inside = -(y0 * w0 + y1 * w1 + y2 * w2)
+            order = (0, 0, 1, 0, 2, 1)
+            sq = pack(stack([-2.0 * y0, -2.0 * y1, -2.0 * y2, norm, 1.0]), order)
+            pr = pack(stack([w0, w1, w2, inside]), order)
             count = (cntw[side, 0, inner] + 127) // 128
             for b in range(chunks):
                 src_sq[offset + b] = sq[:, b * 128 : (b + 1) * 128]
@@ -239,9 +261,9 @@
             return offset + count
 
         end = lax.fori_loop(0, used[c] + 1, slot_body, 0)
-        rows = lax.broadcasted_iota(jnp.int32, (48, 128), 0)
+        pad_rows = lax.broadcasted_iota(jnp.int32, (48, 128), 0)
         for b in range(3):
-            src_sq[end + b] = jnp.where(rows == 3, 1.0, 0.0).astype(BF16)
+            src_sq[end + b] = jnp.where(pad_rows == 3, 1.0, 0.0).astype(BF16)
             src_pr[end + b] = jnp.zeros((48, 128), BF16)
 
         def products(block, sq_ref, pr_ref):
@@ -296,16 +318,12 @@
     near,
     densw,
     kry,
-    maps,
-    ups,
-    fars,
-    nxt,
-    hess,
     maps_v,
     ups_v,
     fars_v,
+    nxt,
+    hess,
     red,
-    local_sem,
     send_sem,
     recv_sem,
 ):
@@ -314,16 +332,6 @@
     coeffs = maps_v.shape[1]
     kinds = fars_v.shape[1]
     window = SIDES * local
-    far_copies = [
-        pltpu.make_async_copy(fars.at[level], fars_v.at[level], local_sem.at[level])
-        for level in range(2)
-    ]
-    up_copy = pltpu.make_async_copy(ups, ups_v, local_sem.at[2])
-    map_copy = pltpu.make_async_copy(maps, maps_v, local_sem.at[3])
-    far_copies[1].start()
-    far_copies[0].start()
-    up_copy.start()
-    map_copy.start()
     barrier = greet(me, total, devs)
 
     groups = gmall[...].reshape(total, coeffs)
@@ -347,34 +355,31 @@
         for o in range(kinds):
             hots[o] = hots[o] + jnp.where(hit & (kind == o), 1.0, 0.0)
     hot = jnp.concatenate(hots, axis=0).astype(BF16)
-    summed = mm(hot, momw[...].reshape(window, coeffs).astype(BF16), NN)
-
-    far_copies[1].wait()
+    held = jnp.concatenate([momw[side].astype(F32) for side in range(SIDES)], axis=0)
+    summed = mm(hot, held.astype(BF16), NN)
+
     g_parts = jnp.zeros((kinds, coeffs), F32)
     for o in range(kinds):
         found = mm(g_both, fars_v[1, o], NT)
         found = found[:kinds] + found[kinds:]
         g_parts = jnp.where(row_is(found.shape, o), found, g_parts)
     g_local = jnp.sum(g_parts, axis=0, keepdims=True).astype(BF16)
-    far_copies[0].wait()
     leaf = jnp.zeros((local, coeffs), F32)
     for o in range(kinds):
         found = mm(halves(summed[o * local : (o + 1) * local]), fars_v[0, o], NT)
         leaf = leaf + found[:local] + found[local:]
-    up_copy.wait()
     g_wide = jnp.broadcast_to(g_local.astype(F32), (local, coeffs)).astype(BF16)
     down = jnp.zeros((local, coeffs), F32)
     for k in range(local):
         found = mm(g_wide, ups_v[k], NN)
         down = jnp.where(row_is(found.shape, k), found, down)
     leaf = (leaf + down).astype(BF16)
-    map_copy.wait()
     far = jnp.zeros((local, panels), F32)
     for c in range(local):
         found = mm(leaf, maps_v[c], NN)
         far = jnp.where(row_is(found.shape, c), found, far)
     live = live_mask(cnt, (local, panels))
-    image = jnp.where(live, 0.5 * densw[RADIUS] + near[...] + far, 0.0)
+    image = jnp.where(live, 0.5 * densw[RADIUS].astype(F32) + near[...] + far, 0.0)
 
     lane = lax.broadcasted_iota(jnp.int32, (1, 128), 1)
     count = kry.shape[0]
@@ -423,7 +428,7 @@
         energy = energy - c_k * c_k
     height = jnp.sqrt(energy + EPSILON)
     nxt[...] = rest / height
-    hess[...] = jnp.where(lane == count, height, sums)
+    hess[...] = jnp.where(lane == count, height, sums)[:, : count + 1]
 
 
 def shards(
@@ -450,40 +455,44 @@
     total = roles * devs
     vmem = pl.BlockSpec(memory_space=pltpu.VMEM)
     smem = pl.BlockSpec(memory_space=pltpu.SMEM)
-    hbm = pl.BlockSpec(memory_space=pl.ANY)
+    hbm = pl.BlockSpec(memory_space=pltpu.HBM)
     dma = pltpu.SemaphoreType.DMA
-    paw, cntw, densw, momw, gmall = pl.pallas_call(
+    posw, anw, cntw, densw, momw, gmall = pl.pallas_call(
         functools.partial(source_kernel, roles, devs),
         name="sources",
         out_shape=(
-            jax.ShapeDtypeStruct((SIDES, local, 6, panels), F32),
+            jax.ShapeDtypeStruct((SIDES, 3, local, panels), F32),
+            jax.ShapeDtypeStruct((SIDES, 3 * local, panels), BF16),
             jax.ShapeDtypeStruct((SIDES, 1, 128), jnp.int32),
-            jax.ShapeDtypeStruct((SIDES, local, panels), F32),
-            jax.ShapeDtypeStruct((SIDES, local, coeffs), F32),
+            jax.ShapeDtypeStruct((SIDES, local, panels), BF16),
+            jax.ShapeDtypeStruct((SIDES, local, coeffs), BF16),
             jax.ShapeDtypeStruct((total, 1, coeffs), F32),
         ),
-        in_specs=[smem, vmem, vmem, vmem, vmem, hbm, hbm, hbm],
-        out_specs=(vmem,) * 5,
+        in_specs=[smem] + [hbm] * 7,
+        out_specs=(vmem,) * 6,
         scratch_shapes=[
+            pltpu.VMEM((3, local, panels), F32),
+            pltpu.VMEM((local, panels), F32),
+            pltpu.VMEM((local, panels), F32),
             pltpu.VMEM(block_inverse.shape, BF16),
             pltpu.VMEM(moment_maps.shape, BF16),
             pltpu.VMEM(up_operators.shape, BF16),
-            dma((2,)),
+            dma((6,)),
             dma((local,)),
-            dma((4, 6)),
-            dma((4, 6)),
+            dma((5, 6)),
+            dma((5, 6)),
             dma((total,)),
             dma((total,)),
         ],
         compiler_params=pltpu.CompilerParams(
-            collective_id=0, has_side_effects=True, vmem_limit_bytes=20 << 20
+            collective_id=0, has_side_effects=True, vmem_limit_bytes=62 << 20
         ),
     )(
         panel_counts,
-        positions,
-        normals,
+        jnp.transpose(positions, (1, 0, 2)),
+        jnp.transpose(normals, (1, 0, 2)),
         panel_areas,
-        krylov_basis[-1],
+        krylov_basis,
         block_inverse,
         moment_maps,
         up_operators,
@@ -494,41 +503,42 @@
     near = pl.pallas_call(
         near_kernel,
         name="near",
+        cost_estimate=pl.CostEstimate(
+            flops=40 * local * panels * panels * (near_lists.shape[1] + 1),
+            bytes_accessed=48 * local * panels * SIDES,
+            transcendentals=local * panels * panels * (near_lists.shape[1] + 1),
+        ),
         out_shape=jax.ShapeDtypeStruct((local, panels), F32),
-        in_specs=[smem, smem, smem, smem, vmem, vmem],
+        in_specs=[smem, smem, smem, smem, vmem, vmem, vmem],
         out_specs=vmem,
         scratch_shapes=[
             pltpu.VMEM((room, 48, 128), BF16),
             pltpu.VMEM((room, 48, 128), BF16),
-            pltpu.VMEM((8, panels), F32),
+            pltpu.VMEM((SIDES, 3, local, panels), F32),
             pltpu.VMEM((JB, panels), F32),
             pltpu.VMEM((JB, panels), F32),
             pltpu.VMEM((JB, panels), F32),
             pltpu.VMEM((JB, panels), F32),
             pltpu.VMEM((8, panels), F32),
         ],
-        compiler_params=pltpu.CompilerParams(vmem_limit_bytes=20 << 20),
-    )(first, near_lists, near_counts, cntw, paw, densw)
+        compiler_params=pltpu.CompilerParams(vmem_limit_bytes=10 << 20),
+    )(first, near_lists, near_counts, cntw, posw, anw, densw)
     nxt, hess = pl.pallas_call(
         functools.partial(finish_kernel, roles, devs),
         name="finish",
         out_shape=(
             jax.ShapeDtypeStruct((local, panels), F32),
-            jax.ShapeDtypeStruct((1, 128), F32),
+            jax.ShapeDtypeStruct((1, krylov_basis.shape[0] + 1), F32),
         ),
-        in_specs=[smem, smem, smem] + [vmem] * 7 + [hbm] * 3,
+        in_specs=[smem, smem, smem] + [vmem] * 10,
         out_specs=(vmem, vmem),
         scratch_shapes=[
-            pltpu.VMEM(moment_maps.shape, BF16),
-            pltpu.VMEM(up_operators.shape, BF16),
-            pltpu.VMEM(far_operators.shape, BF16),
             pltpu.VMEM((total, 1, 128), F32),
-            dma((4,)),
             dma((total,)),
             dma((total,)),
         ],
         compiler_params=pltpu.CompilerParams(
-            collective_id=1, has_side_effects=True, vmem_limit_bytes=20 << 20
+            collective_id=1, has_side_effects=True, vmem_limit_bytes=14 << 20
         ),
     )(
         panel_counts,
@@ -545,7 +555,7 @@
         up_operators,
         far_operators,
     )
-    return nxt, hess[0, : krylov_basis.shape[0] + 1]
+    return nxt, jnp.reshape(hess, (krylov_basis.shape[0] + 1,))
 
 
 def solution(mesh):

time: 70.7 us -> 57.2 us (0.81)
  local copies, waits for them, and re-layouts: 13.6 us -> 4.57 us
  Pallas kernels: 54.9 us -> 50.7 us
    unnamed x39 -> x38, local copies, waits for them, and re-layouts: 12.4 us -> 4.57 us
    pallas_call x1, Pallas kernels: 24.8 us -> 19.3 us  [shards(): pl.pallas_call(functools.partial(source_kernel, roles, devs), name='sourc...]
    pallas_call x1, Pallas kernels: 10.9 us -> 14.1 us  [shards(): pl.pallas_call(functools.partial(finish_kernel, roles, devs), name='finis...]
    pallas_call x1, Pallas kernels: 19.2 us -> 17.4 us  [shards(): pl.pallas_call(near_kernel, name='near', cost_estimate=pl.CostEstimate(fl...]
    squeeze x2 -> x0, local copies, waits for them, and re-layouts: 1.24 us -> none  [the longest x1 0.72 us: shards(): krylov_basis[-1]]
where the time goes in v2:
time: 57.2 us; the launch traced here: 56.1 us
  Pallas kernels  50.7 us (89%)
  local copies, waits for them, and re-layouts  4.57 us (8%)
  between operations  0.86 us (2%)
    pallas_call x1, Pallas kernels, shards(): pl.pallas_call(functools.partial(source_kernel, roles, devs), name='sourc...  19.3 us
    pallas_call x1, Pallas kernels, shards(): pl.pallas_call(near_kernel, name='near', cost_estimate=pl.CostEstimate(fl...  17.4 us
    pallas_call x1, Pallas kernels, shards(): pl.pallas_call(functools.partial(finish_kernel, roles, devs), name='finis...  14.1 us
    unnamed x38, local copies, waits for them, and re-layouts  4.57 us

profile of v2, /device:TPU:0, one launch (start us, length us, event | category | flops | bytes accessed | tf_op | source)
XLA Modules:
  0.0 56.1 jit_solution(7742591764748480072)
XLA Ops:
  0.6 0.0 copy-start.15
  0.6 0.0 copy-start.17
  0.7 19.3 %sources.1 = (f32[7,3,8,512]{3,2,1,0:T(8,128)}, bf16[7,24,512]{2,1,0:T(8,128)(2,1)}, s32[7,1,128]{2,1,0:T(1,128)}, bf16[7,8,512]{2,1,0:T(8,128)(2,1)}, bf16[7,8,...) custom-call(s32[8]{0:T(128)} %cnt.3, f32[3,8,512]{2,1,0:T(8,128)} %bitcast.5, f32[3,8,512]{2,1,0:T(8,128)} %bitcast.6, ...), custom_call_target="tpu_custom_call" | custom-call | tf_op jit(solution)/shard_map/sources/pallas_call | solution.py:460
  20.0 0.0 copy-done.15
  20.0 0.0 copy-done.17
  20.0 0.0 copy-start.4
  20.0 0.8 %copy-done.4 = bf16[7,8,512]{2,1,0:T(8,128)(2,1)S(1)} copy-done((bf16[7,8,512]{2,1,0:T(8,128)(2,1)S(1)}, bf16[7,8,512]{2,1,0:T(8,128)(2,1)}, u32[]{:S(2)}) %copy-start.4) | copy-done | bytes 57368
  20.8 0.0 copy-start.13
  20.8 1.0 %copy-done.13 = f32[7,3,8,512]{3,2,1,0:T(8,128)S(1)} copy-done((f32[7,3,8,512]{3,2,1,0:T(8,128)S(1)}, f32[7,3,8,512]{3,2,1,0:T(8,128)}, u32[]{:S(2)}) %copy-start.13) | copy-done | bytes 344088
  21.8 0.0 copy-start.14
  21.8 0.9 %copy-done.14 = bf16[7,24,512]{2,1,0:T(8,128)(2,1)S(1)} copy-done((bf16[7,24,512]{2,1,0:T(8,128)(2,1)S(1)}, bf16[7,24,512]{2,1,0:T(8,128)(2,1)}, u32[]{:S(2)}) %copy-start.14) | copy-done | bytes 172056
  22.7 0.0 copy-start.16
  22.7 0.7 %copy-done.16 = s32[7,1,128]{2,1,0:T(1,128)S(1)} copy-done((s32[7,1,128]{2,1,0:T(1,128)S(1)}, s32[7,1,128]{2,1,0:T(1,128)}, u32[]{:S(2)}) %copy-start.16) | copy-done | bytes 3608
  23.4 0.0 copy-start
  23.4 0.0 copy-start.1
  23.4 0.0 copy-start.2
  23.4 0.0 copy-start.3
  23.4 0.0 copy-start.5
  23.4 0.0 copy-start.6
  23.4 0.0 copy-start.7
  23.4 0.0 copy-start.8
  23.4 0.0 copy-start.9
  23.4 0.0 copy-start.10
  23.4 0.0 copy-start.11
  23.5 0.0 copy-start.12
  23.5 17.4 %near.2 = f32[8,512]{1,0:T(8,128)S(1)} custom-call(s32[1]{0:T(128)} %bitcast.2.first, s32[8,6]{1,0:T(8,128)S(1)} %copy-done.15, s32[8]{0:T(128)S(1)} %copy-done.17, s32[7,1,128]{2,1,0:T(1,128)S(1)} %copy-done.16, f32[7,3,8,512]{3,2,1,0:T(8,128)S(1)} %copy-done.13, bf16[7,24,512]{2,1,0:T(8,128)(2,1)S(1)} %copy-done.14, bf16[7,8,512]{2,1,0:T(8,128)(2,1)S(1)} %copy-done.4), custom_call_target="tpu_custom_call" | custom-call | flops 587202560 | bytes 1376256 | tf_op jit(solution)/shard_map/near/pallas_call | solution.py:503
  40.8 0.0 copy-done
  40.8 0.0 copy-done.1
  40.9 0.0 copy-done.2
  40.9 0.0 copy-done.3
  40.9 0.0 copy-done.5
  40.9 0.0 copy-done.6
  40.9 0.0 copy-done.7
  40.9 0.0 copy-done.8
  40.9 0.0 copy-done.9
  40.9 0.0 copy-done.10
  40.9 0.0 copy-done.11
  40.9 0.0 copy-done.12
  41.0 14.1 %finish.1 = (f32[8,512]{1,0:T(8,128)S(1)}, f32[1,9]{1,0:T(1,128)S(1)}) custom-call(s32[8]{0:T(128)S(1)} %copy-done.10, s32[1,16]{1,0:T(1,128)S(1)} %copy-done.11, s32[1,16]{1,0:T(1,128)S(1)} %copy-done.12, s32[8,16]{1,0:T(8,128)S(1)} %copy-done.8, s32[8,16]{1,0:T(8,128)S(1)} %copy-done.9, bf16[7,8,256]{2,1,0:T(8,128)(2,1)S(1)} %copy-done.7, ...), custom_call_target="tpu_custom_call" | custom-call | tf_op jit(solution)/shard_map/finish/pallas_call | solution.py:526
  55.0 0.6 %copy.19 = f32[8,512]{1,0:T(8,128)} copy(f32[8,512]{1,0:T(8,128)S(1)} %get-tuple-element.20) | data formatting | bytes 32768
  55.6 0.5 copy.20
Async XLA Ops:
  0.6 19.3 %copy-start.15 = (s32[8,6]{1,0:T(8,128)S(1)}, s32[8,6]{1,0:T(8,128)}, u32[]{:S(2)}) copy-start(s32[8,6]{1,0:T(8,128)} %near.3) | copy-start | bytes 580
  0.6 19.3 %copy-start.17 = (s32[8]{0:T(128)S(1)}, s32[8]{0:T(128)}, u32[]{:S(2)}) copy-start(s32[8]{0:T(128)} %used.1) | copy-start | bytes 100
  20.0 0.8 %copy-start.4 = (bf16[7,8,512]{2,1,0:T(8,128)(2,1)S(1)}, bf16[7,8,512]{2,1,0:T(8,128)(2,1)}, u32[]{:S(2)}) copy-start(bf16[7,8,512]{2,1,0:T(8,128)(2,1)} %get-tuple-element.15.densw) | copy-start | bytes 172036
  20.8 1.0 %copy-start.13 = (f32[7,3,8,512]{3,2,1,0:T(8,128)S(1)}, f32[7,3,8,512]{3,2,1,0:T(8,128)}, u32[]{:S(2)}) copy-start(f32[7,3,8,512]{3,2,1,0:T(8,128)} %get-tuple-element.13.posw) | copy-start | bytes 1032196
  21.8 0.9 %copy-start.14 = (bf16[7,24,512]{2,1,0:T(8,128)(2,1)S(1)}, bf16[7,24,512]{2,1,0:T(8,128)(2,1)}, u32[]{:S(2)}) copy-start(bf16[7,24,512]{2,1,0:T(8,128)(2,1)} %get-tuple-element.14.anw) | copy-start | bytes 516100
  22.7 0.7 %copy-start.16 = (s32[7,1,128]{2,1,0:T(1,128)S(1)}, s32[7,1,128]{2,1,0:T(1,128)}, u32[]{:S(2)}) copy-start(s32[7,1,128]{2,1,0:T(1,128)} %get-tuple-element.12.cntw) | copy-start | bytes 10756
  23.4 17.5 %copy-start = (bf16[8,256,512]{2,1,0:T(8,128)(2,1)S(1)}, bf16[8,256,512]{2,1,0:T(8,128)(2,1)}, u32[]{:S(2)}) copy-start(bf16[8,256,512]{2,1,0:T(8,128)(2,1)} %maps_v.1) | copy-start | bytes 6291460
  23.4 17.5 %copy-start.1 = (bf16[8,256,256]{2,1,0:T(8,128)(2,1)S(1)}, bf16[8,256,256]{2,1,0:T(8,128)(2,1)}, u32[]{:S(2)}) copy-start(bf16[8,256,256]{2,1,0:T(8,128)(2,1)} %ups_v.1) | copy-start | bytes 3145732
  23.4 17.5 %copy-start.2 = (bf16[2,8,256,256]{3,2,1,0:T(8,128)(2,1)S(1)}, bf16[2,8,256,256]{3,2,1,0:T(8,128)(2,1)}, u32[]{:S(2)}) copy-start(bf16[2,8,256,256]{3,2,1,0:T(8,128)(2,1)} %fars_v.1) | copy-start | bytes 6291460
  23.4 17.5 %copy-start.3 = (f32[8,8,512]{2,1,0:T(8,128)S(1)}, f32[8,8,512]{2,1,0:T(8,128)}, u32[]{:S(2)}) copy-start(f32[8,8,512]{2,1,0:T(8,128)} %kry.3) | copy-start | bytes 393220
  23.4 17.5 %copy-start.5 = (bf16[7,8,512]{2,1,0:T(8,128)(2,1)S(1)}, bf16[7,8,512]{2,1,0:T(8,128)(2,1)}, u32[]{:S(2)}) copy-start(bf16[7,8,512]{2,1,0:T(8,128)(2,1)} %get-tuple-element.15.densw) | copy-start | bytes 172036
  23.4 17.5 %copy-start.6 = (f32[32,1,256]{2,1,0:T(1,128)S(1)}, f32[32,1,256]{2,1,0:T(1,128)}, u32[]{:S(2)}) copy-start(f32[32,1,256]{2,1,0:T(1,128)} %get-tuple-element.11.gmall) | copy-start | bytes 98308
  23.4 17.5 %copy-start.7 = (bf16[7,8,256]{2,1,0:T(8,128)(2,1)S(1)}, bf16[7,8,256]{2,1,0:T(8,128)(2,1)}, u32[]{:S(2)}) copy-start(bf16[7,8,256]{2,1,0:T(8,128)(2,1)} %get-tuple-element.10.momw) | copy-start | bytes 86020
  23.4 17.5 %copy-start.8 = (s32[8,16]{1,0:T(8,128)S(1)}, s32[8,16]{1,0:T(8,128)}, u32[]{:S(2)}) copy-start(s32[8,16]{1,0:T(8,128)} %llist.1) | copy-start | bytes 1540
  23.4 17.5 %copy-start.9 = (s32[8,16]{1,0:T(8,128)S(1)}, s32[8,16]{1,0:T(8,128)}, u32[]{:S(2)}) copy-start(s32[8,16]{1,0:T(8,128)} %lkind.1) | copy-start | bytes 1540
  23.4 17.5 %copy-start.10 = (s32[8]{0:T(128)S(1)}, s32[8]{0:T(128)}, u32[]{:S(2)}) copy-start(s32[8]{0:T(128)} %cnt.3) | copy-start | bytes 100
  23.4 17.5 %copy-start.11 = (s32[1,16]{1,0:T(1,128)S(1)}, s32[1,16]{1,0:T(1,128)}, u32[]{:S(2)}) copy-start(s32[1,16]{1,0:T(1,128)} %glist.1) | copy-start | bytes 196
  23.5 17.5 %copy-start.12 = (s32[1,16]{1,0:T(1,128)S(1)}, s32[1,16]{1,0:T(1,128)}, u32[]{:S(2)}) copy-start(s32[1,16]{1,0:T(1,128)} %gkind.1) | copy-start | bytes 196

commit v3 on v2

--- a/solution.py
+++ b/solution.py
@@ -210,7 +210,7 @@
 
 
 def near_kernel(
-    first, near, used, cntw, posw, anw, densw, out, src_sq, src_pr, weight, sq0, pr0, sq1, pr1, acc
+    first, near, used, cntw, posw, anw, densw, out, src_sq, src_pr, weight, target_v, result, sq0, pr0, sq1, pr1, acc
 ):
     local, panels = out.shape
     chunks = panels // 128
@@ -266,43 +266,54 @@
             src_sq[end + b] = jnp.where(pad_rows == 3, 1.0, 0.0).astype(BF16)
             src_pr[end + b] = jnp.zeros((48, 128), BF16)
 
-        def products(block, sq_ref, pr_ref):
-            for half in range(2):
-                part = pl.ds(half * 128, 128)
-                sq_ref[part, :] = mm(src_sq[2 * block + half], target, TN)
-                pr_ref[part, :] = mm(src_pr[2 * block + half], target, TN)
-
-        def consume(sq_ref, pr_ref):
-            for r in range(0, panels, 256):
-                total = acc[:, r : r + 256]
+        blocks = (end + 1) // 2
+        wide = target_v.shape[2]
+        for h in range(target_v.shape[0]):
+            target_v[h] = target[:, h * wide : (h + 1) * wide]
+
+        def half_body(h, carry):
+            aim = target_v[h]
+
+            def products(block, sq_ref, pr_ref):
+                for half in range(2):
+                    part = pl.ds(half * 128, 128)
+                    sq_ref[part, :] = mm(src_sq[2 * block + half], aim, TN)
+                    pr_ref[part, :] = mm(src_pr[2 * block + half], aim, TN)
+
+            def consume(sq_ref, pr_ref):
+                total = acc[...]
                 for j in range(0, JB, 8):
-                    inverse = lax.rsqrt(sq_ref[j : j + 8, r : r + 256])
-                    total = total + pr_ref[j : j + 8, r : r + 256] * inverse * (
-                        inverse * inverse
-                    )
-                acc[:, r : r + 256] = total
-
-        acc[...] = jnp.zeros(acc.shape, F32)
-        blocks = (end + 1) // 2
-        products(0, sq0, pr0)
-
-        def pair_body(t, carry):
-            products(2 * t + 1, sq1, pr1)
-            consume(sq0, pr0)
-            products(2 * t + 2, sq0, pr0)
-            consume(sq1, pr1)
+                    inverse = lax.rsqrt(sq_ref[j : j + 8, :])
+                    total = total + pr_ref[j : j + 8, :] * inverse * (inverse * inverse)
+                acc[...] = total
+
+            acc[...] = jnp.zeros(acc.shape, F32)
+            products(0, sq0, pr0)
+
+            def pair_body(t, inner_carry):
+                products(2 * t + 1, sq1, pr1)
+                consume(sq0, pr0)
+                products(2 * t + 2, sq0, pr0)
+                consume(sq1, pr1)
+                return inner_carry
+
+            lax.fori_loop(0, blocks // 2, pair_body, 0)
+
+            @pl.when(lax.rem(blocks, 2) == 1)
+            def _():
+                consume(sq0, pr0)
+
+            result[h, pl.ds(c, 1), :] = jnp.sum(acc[...], axis=0, keepdims=True)
             return carry
 
-        lax.fori_loop(0, blocks // 2, pair_body, 0)
-
-        @pl.when(lax.rem(blocks, 2) == 1)
-        def _():
-            consume(sq0, pr0)
-
-        out[pl.ds(c, 1), :] = jnp.sum(acc[...], axis=0, keepdims=True)
+        lax.fori_loop(0, (cntw[RADIUS, 0, c] + wide - 1) // wide, half_body, 0)
         return carry
 
+    result[...] = jnp.zeros(result.shape, F32)
     lax.fori_loop(0, local, cluster_body, 0)
+    for h in range(result.shape[0]):
+        wide = result.shape[2]
+        out[:, h * wide : (h + 1) * wide] = result[h]
 
 
 def finish_kernel(
@@ -499,6 +510,7 @@
     )
     own = lax.axis_index(AXES)
     first = jnp.reshape((own - RADIUS) * local, (1,)).astype(jnp.int32)
+    wide = min(256, panels)
     room = (near_lists.shape[1] + 1) * (panels // 128) + 8
     near = pl.pallas_call(
         near_kernel,
@@ -515,11 +527,13 @@
             pltpu.VMEM((room, 48, 128), BF16),
             pltpu.VMEM((room, 48, 128), BF16),
             pltpu.VMEM((SIDES, 3, local, panels), F32),
-            pltpu.VMEM((JB, panels), F32),
-            pltpu.VMEM((JB, panels), F32),
-            pltpu.VMEM((JB, panels), F32),
-            pltpu.VMEM((JB, panels), F32),
-            pltpu.VMEM((8, panels), F32),
+            pltpu.VMEM((panels // wide, 48, wide), BF16),
+            pltpu.VMEM((panels // wide, local, wide), F32),
+            pltpu.VMEM((JB, wide), F32),
+            pltpu.VMEM((JB, wide), F32),
+            pltpu.VMEM((JB, wide), F32),
+            pltpu.VMEM((JB, wide), F32),
+            pltpu.VMEM((8, wide), F32),
         ],
         compiler_params=pltpu.CompilerParams(vmem_limit_bytes=10 << 20),
     )(first, near_lists, near_counts, cntw, posw, anw, densw)

time: 57.2 us -> 60.1 us (1.051); the launches traced: 56.1 us -> 60.3 us
  Pallas kernels: 50.7 us -> 54.9 us
    pallas_call x1, Pallas kernels: 17.4 us -> 20.5 us  [shards(): pl.pallas_call(near_kernel, name='near', cost_estimate=pl.CostEstimate(fl...]
    pallas_call x1, Pallas kernels: 14.1 us -> 15.1 us  [shards(): pl.pallas_call(functools.partial(finish_kernel, roles, devs), name='finis...]
where the time goes in v3:
time: 60.1 us; the launch traced here: 60.3 us
  Pallas kernels  54.9 us (91%)
  local copies, waits for them, and re-layouts  4.57 us (8%)
  between operations  0.86 us (1%)
    pallas_call x1, Pallas kernels, shards(): pl.pallas_call(near_kernel, name='near', cost_estimate=pl.CostEstimate(fl...  20.5 us
    pallas_call x1, Pallas kernels, shards(): pl.pallas_call(functools.partial(source_kernel, roles, devs), name='sourc...  19.3 us
    pallas_call x1, Pallas kernels, shards(): pl.pallas_call(functools.partial(finish_kernel, roles, devs), name='finis...  15.1 us
    unnamed x38, local copies, waits for them, and re-layouts  4.57 us

profile of v3, /device:TPU:0, one launch (start us, length us, event | category | flops | bytes accessed | tf_op | source)
XLA Modules:
  0.0 60.3 jit_solution(18285638718585710902)
XLA Ops:
  0.6 0.0 copy-start.15
  0.6 0.0 copy-start.17
  0.7 19.3 %sources.1 = (f32[7,3,8,512]{3,2,1,0:T(8,128)}, bf16[7,24,512]{2,1,0:T(8,128)(2,1)}, s32[7,1,128]{2,1,0:T(1,128)}, bf16[7,8,512]{2,1,0:T(8,128)(2,1)}, bf16[7,8,...) custom-call(s32[8]{0:T(128)} %cnt.3, f32[3,8,512]{2,1,0:T(8,128)} %bitcast.5, f32[3,8,512]{2,1,0:T(8,128)} %bitcast.6, ...), custom_call_target="tpu_custom_call" | custom-call | tf_op jit(solution)/shard_map/sources/pallas_call | solution.py:471
  20.0 0.0 copy-done.15
  20.0 0.0 copy-done.17
  20.0 0.0 copy-start.4
  20.0 0.8 %copy-done.4 = bf16[7,8,512]{2,1,0:T(8,128)(2,1)S(1)} copy-done((bf16[7,8,512]{2,1,0:T(8,128)(2,1)S(1)}, bf16[7,8,512]{2,1,0:T(8,128)(2,1)}, u32[]{:S(2)}) %copy-start.4) | copy-done | bytes 57368
  20.8 0.0 copy-start.13
  20.8 1.0 %copy-done.13 = f32[7,3,8,512]{3,2,1,0:T(8,128)S(1)} copy-done((f32[7,3,8,512]{3,2,1,0:T(8,128)S(1)}, f32[7,3,8,512]{3,2,1,0:T(8,128)}, u32[]{:S(2)}) %copy-start.13) | copy-done | bytes 344088
  21.8 0.0 copy-start.14
  21.8 0.9 %copy-done.14 = bf16[7,24,512]{2,1,0:T(8,128)(2,1)S(1)} copy-done((bf16[7,24,512]{2,1,0:T(8,128)(2,1)S(1)}, bf16[7,24,512]{2,1,0:T(8,128)(2,1)}, u32[]{:S(2)}) %copy-start.14) | copy-done | bytes 172056
  22.7 0.0 copy-start.16
  22.7 0.7 %copy-done.16 = s32[7,1,128]{2,1,0:T(1,128)S(1)} copy-done((s32[7,1,128]{2,1,0:T(1,128)S(1)}, s32[7,1,128]{2,1,0:T(1,128)}, u32[]{:S(2)}) %copy-start.16) | copy-done | bytes 3608
  23.4 0.0 copy-start
  23.4 0.0 copy-start.1
  23.4 0.0 copy-start.2
  23.4 0.0 copy-start.3
  23.4 0.0 copy-start.5
  23.4 0.0 copy-start.6
  23.4 0.0 copy-start.7
  23.4 0.0 copy-start.8
  23.4 0.0 copy-start.9
  23.4 0.0 copy-start.10
  23.4 0.0 copy-start.11
  23.5 0.0 copy-start.12
  23.5 20.5 %near.2 = f32[8,512]{1,0:T(8,128)S(1)} custom-call(s32[1]{0:T(128)} %bitcast.2.first, s32[8,6]{1,0:T(8,128)S(1)} %copy-done.15, s32[8]{0:T(128)S(1)} %copy-done.17, s32[7,1,128]{2,1,0:T(1,128)S(1)} %copy-done.16, f32[7,3,8,512]{3,2,1,0:T(8,128)S(1)} %copy-done.13, bf16[7,24,512]{2,1,0:T(8,128)(2,1)S(1)} %copy-done.14, bf16[7,8,512]{2,1,0:T(8,128)(2,1)S(1)} %copy-done.4), custom_call_target="tpu_custom_call" | custom-call | flops 587202560 | bytes 1376256 | tf_op jit(solution)/shard_map/near/pallas_call | solution.py:515
  43.9 0.0 copy-done
  44.0 0.0 copy-done.1
  44.0 0.0 copy-done.2
  44.0 0.0 copy-done.3
  44.0 0.0 copy-done.5
  44.0 0.0 copy-done.6
  44.0 0.0 copy-done.7
  44.0 0.0 copy-done.8
  44.0 0.0 copy-done.9
  44.0 0.0 copy-done.10
  44.0 0.0 copy-done.11
  44.1 0.0 copy-done.12
  44.1 15.1 %finish.1 = (f32[8,512]{1,0:T(8,128)S(1)}, f32[1,9]{1,0:T(1,128)S(1)}) custom-call(s32[8]{0:T(128)S(1)} %copy-done.10, s32[1,16]{1,0:T(1,128)S(1)} %copy-done.11, s32[1,16]{1,0:T(1,128)S(1)} %copy-done.12, s32[8,16]{1,0:T(8,128)S(1)} %copy-done.8, s32[8,16]{1,0:T(8,128)S(1)} %copy-done.9, bf16[7,8,256]{2,1,0:T(8,128)(2,1)S(1)} %copy-done.7, ...), custom_call_target="tpu_custom_call" | custom-call | tf_op jit(solution)/shard_map/finish/pallas_call | solution.py:540
  59.2 0.6 %copy.19 = f32[8,512]{1,0:T(8,128)} copy(f32[8,512]{1,0:T(8,128)S(1)} %get-tuple-element.20) | data formatting | bytes 32768
  59.8 0.5 copy.20
Async XLA Ops:
  0.6 19.3 %copy-start.15 = (s32[8,6]{1,0:T(8,128)S(1)}, s32[8,6]{1,0:T(8,128)}, u32[]{:S(2)}) copy-start(s32[8,6]{1,0:T(8,128)} %near.3) | copy-start | bytes 580
  0.6 19.3 %copy-start.17 = (s32[8]{0:T(128)S(1)}, s32[8]{0:T(128)}, u32[]{:S(2)}) copy-start(s32[8]{0:T(128)} %used.1) | copy-start | bytes 100
  20.0 0.8 %copy-start.4 = (bf16[7,8,512]{2,1,0:T(8,128)(2,1)S(1)}, bf16[7,8,512]{2,1,0:T(8,128)(2,1)}, u32[]{:S(2)}) copy-start(bf16[7,8,512]{2,1,0:T(8,128)(2,1)} %get-tuple-element.15.densw) | copy-start | bytes 172036
  20.8 1.0 %copy-start.13 = (f32[7,3,8,512]{3,2,1,0:T(8,128)S(1)}, f32[7,3,8,512]{3,2,1,0:T(8,128)}, u32[]{:S(2)}) copy-start(f32[7,3,8,512]{3,2,1,0:T(8,128)} %get-tuple-element.13.posw) | copy-start | bytes 1032196
  21.8 0.9 %copy-start.14 = (bf16[7,24,512]{2,1,0:T(8,128)(2,1)S(1)}, bf16[7,24,512]{2,1,0:T(8,128)(2,1)}, u32[]{:S(2)}) copy-start(bf16[7,24,512]{2,1,0:T(8,128)(2,1)} %get-tuple-element.14.anw) | copy-start | bytes 516100
  22.7 0.7 %copy-start.16 = (s32[7,1,128]{2,1,0:T(1,128)S(1)}, s32[7,1,128]{2,1,0:T(1,128)}, u32[]{:S(2)}) copy-start(s32[7,1,128]{2,1,0:T(1,128)} %get-tuple-element.12.cntw) | copy-start | bytes 10756
  23.4 20.6 %copy-start = (bf16[8,256,512]{2,1,0:T(8,128)(2,1)S(1)}, bf16[8,256,512]{2,1,0:T(8,128)(2,1)}, u32[]{:S(2)}) copy-start(bf16[8,256,512]{2,1,0:T(8,128)(2,1)} %maps_v.1) | copy-start | bytes 6291460
  23.4 20.6 %copy-start.1 = (bf16[8,256,256]{2,1,0:T(8,128)(2,1)S(1)}, bf16[8,256,256]{2,1,0:T(8,128)(2,1)}, u32[]{:S(2)}) copy-start(bf16[8,256,256]{2,1,0:T(8,128)(2,1)} %ups_v.1) | copy-start | bytes 3145732
  23.4 20.6 %copy-start.2 = (bf16[2,8,256,256]{3,2,1,0:T(8,128)(2,1)S(1)}, bf16[2,8,256,256]{3,2,1,0:T(8,128)(2,1)}, u32[]{:S(2)}) copy-start(bf16[2,8,256,256]{3,2,1,0:T(8,128)(2,1)} %fars_v.1) | copy-start | bytes 6291460
  23.4 20.6 %copy-start.3 = (f32[8,8,512]{2,1,0:T(8,128)S(1)}, f32[8,8,512]{2,1,0:T(8,128)}, u32[]{:S(2)}) copy-start(f32[8,8,512]{2,1,0:T(8,128)} %kry.3) | copy-start | bytes 393220
  23.4 20.6 %copy-start.5 = (bf16[7,8,512]{2,1,0:T(8,128)(2,1)S(1)}, bf16[7,8,512]{2,1,0:T(8,128)(2,1)}, u32[]{:S(2)}) copy-start(bf16[7,8,512]{2,1,0:T(8,128)(2,1)} %get-tuple-element.15.densw) | copy-start | bytes 172036
  23.4 20.6 %copy-start.6 = (f32[32,1,256]{2,1,0:T(1,128)S(1)}, f32[32,1,256]{2,1,0:T(1,128)}, u32[]{:S(2)}) copy-start(f32[32,1,256]{2,1,0:T(1,128)} %get-tuple-element.11.gmall) | copy-start | bytes 98308
  23.4 20.6 %copy-start.7 = (bf16[7,8,256]{2,1,0:T(8,128)(2,1)S(1)}, bf16[7,8,256]{2,1,0:T(8,128)(2,1)}, u32[]{:S(2)}) copy-start(bf16[7,8,256]{2,1,0:T(8,128)(2,1)} %get-tuple-element.10.momw) | copy-start | bytes 86020
  23.4 20.6 %copy-start.8 = (s32[8,16]{1,0:T(8,128)S(1)}, s32[8,16]{1,0:T(8,128)}, u32[]{:S(2)}) copy-start(s32[8,16]{1,0:T(8,128)} %llist.1) | copy-start | bytes 1540
  23.4 20.6 %copy-start.9 = (s32[8,16]{1,0:T(8,128)S(1)}, s32[8,16]{1,0:T(8,128)}, u32[]{:S(2)}) copy-start(s32[8,16]{1,0:T(8,128)} %lkind.1) | copy-start | bytes 1540
  23.4 20.6 %copy-start.10 = (s32[8]{0:T(128)S(1)}, s32[8]{0:T(128)}, u32[]{:S(2)}) copy-start(s32[8]{0:T(128)} %cnt.3) | copy-start | bytes 100
  23.4 20.6 %copy-start.11 = (s32[1,16]{1,0:T(1,128)S(1)}, s32[1,16]{1,0:T(1,128)}, u32[]{:S(2)}) copy-start(s32[1,16]{1,0:T(1,128)} %glist.1) | copy-start | bytes 196
  23.5 20.6 %copy-start.12 = (s32[1,16]{1,0:T(1,128)S(1)}, s32[1,16]{1,0:T(1,128)}, u32[]{:S(2)}) copy-start(s32[1,16]{1,0:T(1,128)} %gkind.1) | copy-start | bytes 196

commit v4 on v2

--- a/solution.py
+++ b/solution.py
@@ -81,7 +81,6 @@
     posw,
     anw,
     cntw,
-    densw,
     momw,
     gmall,
     nrm_v,
@@ -119,7 +118,7 @@
     for copy in small:
         copy.wait()
     parts = [nrm_v[a] * area_v[...] for a in range(3)]
-    anw[RADIUS] = jnp.concatenate(parts, axis=0).astype(BF16)
+    anw[RADIUS, : 3 * local] = jnp.concatenate(parts, axis=0).astype(BF16)
     lane = lax.broadcasted_iota(jnp.int32, (1, 128), 1)
     counts = jnp.zeros((1, 128), jnp.int32)
     for c in range(local):
@@ -127,13 +126,17 @@
     cntw[RADIUS] = counts
     pl.semaphore_wait(barrier, total - 1)
 
-    def to_neighbours(ref, kind):
+    def to_neighbours(ref, kind, rows=None):
         made = []
+
+        def slot(side):
+            return ref.at[side] if rows is None else ref.at[side, rows]
+
         for n, d in enumerate([1, -1, 2, -2, 3, -3]):
             made.append(
                 pltpu.make_async_remote_copy(
-                    src_ref=ref.at[RADIUS],
-                    dst_ref=ref.at[RADIUS - d],
+                    src_ref=slot(RADIUS),
+                    dst_ref=slot(RADIUS - d),
                     send_sem=send_sem.at[kind, n],
                     recv_sem=recv_sem.at[kind, n],
                     device_id=coords(lax.rem(me + d + total, total), devs),
@@ -144,7 +147,7 @@
             copy.start()
         return made
 
-    sent = to_neighbours(posw, 0) + to_neighbours(anw, 4) + to_neighbours(cntw, 1)
+    sent = to_neighbours(posw, 0) + to_neighbours(anw, 4, pl.ds(0, 3 * local)) + to_neighbours(cntw, 1)
     live = live_mask(cnt, (local, panels))
     current = kry_v[...].astype(BF16)
     density = jnp.zeros((local, panels), F32)
@@ -153,8 +156,8 @@
         found = mm(current, binv_v[c], NT)
         density = jnp.where(row_is(found.shape, c), found, density)
     rounded = jnp.where(live, density, 0.0).astype(BF16)
-    densw[RADIUS] = rounded
-    sent += to_neighbours(densw, 2)
+    anw[RADIUS, 3 * local :] = rounded
+    sent += to_neighbours(anw, 2, pl.ds(3 * local, local))
     map_copy.wait()
     moments = jnp.zeros((local, coeffs), F32)
     for c in range(local):
@@ -210,15 +213,15 @@
 
 
 def near_kernel(
-    first, near, used, cntw, posw, anw, densw, out, src_sq, src_pr, weight, sq0, pr0, sq1, pr1, acc
+    first, near, used, cntw, posw, anw, out, src_sq, src_pr, weight, sq0, pr0, sq1, pr1, acc
 ):
     local, panels = out.shape
     chunks = panels // 128
     shape = (8, panels)
     rows = lax.broadcasted_iota(jnp.int32, shape, 0)
     for side in range(SIDES):
-        dens = densw[side].astype(F32)
         products_an = anw[side].astype(F32)
+        dens = products_an[3 * local :]
         for a in range(3):
             weight[side, a] = products_an[a * local : (a + 1) * local] * dens
 
@@ -316,7 +319,7 @@
     momw,
     gmall,
     near,
-    densw,
+    anw,
     kry,
     maps_v,
     ups_v,
@@ -379,7 +382,7 @@
         found = mm(leaf, maps_v[c], NN)
         far = jnp.where(row_is(found.shape, c), found, far)
     live = live_mask(cnt, (local, panels))
-    image = jnp.where(live, 0.5 * densw[RADIUS].astype(F32) + near[...] + far, 0.0)
+    image = jnp.where(live, 0.5 * anw[RADIUS].astype(F32)[3 * local :] + near[...] + far, 0.0)
 
     lane = lax.broadcasted_iota(jnp.int32, (1, 128), 1)
     count = kry.shape[0]
@@ -457,19 +460,18 @@
     smem = pl.BlockSpec(memory_space=pltpu.SMEM)
     hbm = pl.BlockSpec(memory_space=pltpu.HBM)
     dma = pltpu.SemaphoreType.DMA
-    posw, anw, cntw, densw, momw, gmall = pl.pallas_call(
+    posw, anw, cntw, momw, gmall = pl.pallas_call(
         functools.partial(source_kernel, roles, devs),
         name="sources",
         out_shape=(
             jax.ShapeDtypeStruct((SIDES, 3, local, panels), F32),
-            jax.ShapeDtypeStruct((SIDES, 3 * local, panels), BF16),
+            jax.ShapeDtypeStruct((SIDES, 4 * local, panels), BF16),
             jax.ShapeDtypeStruct((SIDES, 1, 128), jnp.int32),
-            jax.ShapeDtypeStruct((SIDES, local, panels), BF16),
             jax.ShapeDtypeStruct((SIDES, local, coeffs), BF16),
             jax.ShapeDtypeStruct((total, 1, coeffs), F32),
         ),
         in_specs=[smem] + [hbm] * 7,
-        out_specs=(vmem,) * 6,
+        out_specs=(vmem,) * 5,
         scratch_shapes=[
             pltpu.VMEM((3, local, panels), F32),
             pltpu.VMEM((local, panels), F32),
@@ -509,7 +511,7 @@
             transcendentals=local * panels * panels * (near_lists.shape[1] + 1),
         ),
         out_shape=jax.ShapeDtypeStruct((local, panels), F32),
-        in_specs=[smem, smem, smem, smem, vmem, vmem, vmem],
+        in_specs=[smem, smem, smem, smem, vmem, vmem],
         out_specs=vmem,
         scratch_shapes=[
             pltpu.VMEM((room, 48, 128), BF16),
@@ -522,7 +524,7 @@
             pltpu.VMEM((8, panels), F32),
         ],
         compiler_params=pltpu.CompilerParams(vmem_limit_bytes=10 << 20),
-    )(first, near_lists, near_counts, cntw, posw, anw, densw)
+    )(first, near_lists, near_counts, cntw, posw, anw)
     nxt, hess = pl.pallas_call(
         functools.partial(finish_kernel, roles, devs),
         name="finish",
@@ -549,7 +551,7 @@
         momw,
         gmall,
         near,
-        densw,
+        anw,
         krylov_basis,
         moment_maps,
         up_operators,

time: 57.2 us -> 54.2 us (0.948)
  Pallas kernels: 50.7 us -> 48.8 us
  local copies, waits for them, and re-layouts: 4.57 us -> 3.77 us
    pallas_call x1, Pallas kernels: 14.1 us -> 9.39 us  [shards(): pl.pallas_call(functools.partial(finish_kernel, roles, devs), name='finis...]
    pallas_call x1, Pallas kernels: 17.4 us -> 20.1 us  [shards(): pl.pallas_call(near_kernel, name='near', cost_estimate=pl.CostEstimate(fl...]
    unnamed x38 -> x36, local copies, waits for them, and re-layouts: 4.57 us -> 3.77 us
where the time goes in v4:
time: 54.2 us; the launch traced here: 53.4 us
  Pallas kernels  48.8 us (90%)
  local copies, waits for them, and re-layouts  3.77 us (7%)
  between operations  0.86 us (2%)
    pallas_call x1, Pallas kernels, shards(): pl.pallas_call(near_kernel, name='near', cost_estimate=pl.CostEstimate(fl...  20.1 us
    pallas_call x1, Pallas kernels, shards(): pl.pallas_call(functools.partial(source_kernel, roles, devs), name='sourc...  19.3 us
    pallas_call x1, Pallas kernels, shards(): pl.pallas_call(functools.partial(finish_kernel, roles, devs), name='finis...  9.39 us
    unnamed x36, local copies, waits for them, and re-layouts  3.77 us

profile of v4, /device:TPU:0, one launch (start us, length us, event | category | flops | bytes accessed | tf_op | source)
XLA Modules:
  0.0 53.4 jit_solution(7071656648161612205)
XLA Ops:
  0.6 0.0 copy-start.14
  0.6 0.0 copy-start.16
  0.7 19.3 %sources.1 = (f32[7,3,8,512]{3,2,1,0:T(8,128)}, bf16[7,32,512]{2,1,0:T(8,128)(2,1)}, s32[7,1,128]{2,1,0:T(1,128)}, bf16[7,8,256]{2,1,0:T(8,128)(2,1)}, f32[32,1,256]{2,1,0:T(1,128)}) custom-call(s32[8]{0:T(128)} %cnt.3, f32[3,8,512]{2,1,0:T(8,128)} %bitcast.5, f32[3,8,512]{2,1,0:T(8,128)} %bitcast.6, f32[8,512]{1,0:T(8,128)} %area.1, f32[8,8,512]{2,1,0:T(8,128)} %kry.3, ...), custom_call_target="tpu_custom_call" | custom-call | tf_op jit(solution)/shard_map/sources/pallas_call | solution.py:463
  20.0 0.0 copy-done.14
  20.0 0.0 copy-done.16
  20.0 0.0 copy-start.4
  20.0 0.9 %copy-done.4 = bf16[7,32,512]{2,1,0:T(8,128)(2,1)S(1)} copy-done((bf16[7,32,512]{2,1,0:T(8,128)(2,1)S(1)}, bf16[7,32,512]{2,1,0:T(8,128)(2,1)}, u32[]{:S(2)}) %copy-start.4) | copy-done | bytes 229400
  20.9 0.0 copy-start.13
  20.9 1.0 %copy-done.13 = f32[7,3,8,512]{3,2,1,0:T(8,128)S(1)} copy-done((f32[7,3,8,512]{3,2,1,0:T(8,128)S(1)}, f32[7,3,8,512]{3,2,1,0:T(8,128)}, u32[]{:S(2)}) %copy-start.13) | copy-done | bytes 344088
  21.9 0.0 copy-start.15
  21.9 0.7 %copy-done.15 = s32[7,1,128]{2,1,0:T(1,128)S(1)} copy-done((s32[7,1,128]{2,1,0:T(1,128)S(1)}, s32[7,1,128]{2,1,0:T(1,128)}, u32[]{:S(2)}) %copy-start.15) | copy-done | bytes 3608
  22.6 0.0 copy-start
  22.6 0.0 copy-start.1
  22.6 0.0 copy-start.2
  22.6 0.0 copy-start.3
  22.6 0.0 copy-start.5
  22.6 0.0 copy-start.6
  22.6 0.0 copy-start.7
  22.6 0.0 copy-start.8
  22.6 0.0 copy-start.9
  22.6 0.0 copy-start.10
  22.7 0.0 copy-start.11
  22.7 0.0 copy-start.12
  22.7 20.1 %near.2 = f32[8,512]{1,0:T(8,128)S(1)} custom-call(s32[1]{0:T(128)} %bitcast.2.first, s32[8,6]{1,0:T(8,128)S(1)} %copy-done.14, s32[8]{0:T(128)S(1)} %copy-done.16, s32[7,1,128]{2,1,0:T(1,128)S(1)} %copy-done.15, f32[7,3,8,512]{3,2,1,0:T(8,128)S(1)} %copy-done.13, bf16[7,32,512]{2,1,0:T(8,128)(2,1)S(1)} %copy-done.4), custom_call_target="tpu_custom_call" | custom-call | flops 587202560 | bytes 1376256 | tf_op jit(solution)/shard_map/near/pallas_call | solution.py:505
  42.8 0.0 copy-done
  42.8 0.0 copy-done.1
  42.8 0.0 copy-done.2
  42.8 0.0 copy-done.3
  42.8 0.0 copy-done.5
  42.8 0.0 copy-done.6
  42.8 0.0 copy-done.7
  42.8 0.0 copy-done.8
  42.8 0.0 copy-done.9
  42.8 0.0 copy-done.10
  42.9 0.0 copy-done.11
  42.9 0.0 copy-done.12
  42.9 9.4 %finish.1 = (f32[8,512]{1,0:T(8,128)S(1)}, f32[1,9]{1,0:T(1,128)S(1)}) custom-call(s32[8]{0:T(128)S(1)} %copy-done.10, s32[1,16]{1,0:T(1,128)S(1)} %copy-done.11, s32[1,16]{1,0:T(1,128)S(1)} %copy-done.12, s32[8,16]{1,0:T(8,128)S(1)} %copy-done.8, s32[8,16]{1,0:T(8,128)S(1)} %copy-done.9, bf16[7,8,256]{2,1,0:T(8,128)(2,1)S(1)} %copy-done.7, ...), custom_call_target="tpu_custom_call" | custom-call | tf_op jit(solution)/shard_map/finish/pallas_call | solution.py:528
  52.3 0.6 %copy.19 = f32[8,512]{1,0:T(8,128)} copy(f32[8,512]{1,0:T(8,128)S(1)} %get-tuple-element.18) | data formatting | bytes 32768
  52.9 0.5 copy.20
Async XLA Ops:
  0.6 19.3 %copy-start.14 = (s32[8,6]{1,0:T(8,128)S(1)}, s32[8,6]{1,0:T(8,128)}, u32[]{:S(2)}) copy-start(s32[8,6]{1,0:T(8,128)} %near.3) | copy-start | bytes 580
  0.6 19.3 %copy-start.16 = (s32[8]{0:T(128)S(1)}, s32[8]{0:T(128)}, u32[]{:S(2)}) copy-start(s32[8]{0:T(128)} %used.1) | copy-start | bytes 100
  20.0 0.9 %copy-start.4 = (bf16[7,32,512]{2,1,0:T(8,128)(2,1)S(1)}, bf16[7,32,512]{2,1,0:T(8,128)(2,1)}, u32[]{:S(2)}) copy-start(bf16[7,32,512]{2,1,0:T(8,128)(2,1)} %get-tuple-element.13.anw) | copy-start | bytes 688132
  20.9 1.0 %copy-start.13 = (f32[7,3,8,512]{3,2,1,0:T(8,128)S(1)}, f32[7,3,8,512]{3,2,1,0:T(8,128)}, u32[]{:S(2)}) copy-start(f32[7,3,8,512]{3,2,1,0:T(8,128)} %get-tuple-element.12.posw) | copy-start | bytes 1032196
  21.9 0.7 %copy-start.15 = (s32[7,1,128]{2,1,0:T(1,128)S(1)}, s32[7,1,128]{2,1,0:T(1,128)}, u32[]{:S(2)}) copy-start(s32[7,1,128]{2,1,0:T(1,128)} %get-tuple-element.11.cntw) | copy-start | bytes 10756
  22.6 20.2 %copy-start = (bf16[8,256,512]{2,1,0:T(8,128)(2,1)S(1)}, bf16[8,256,512]{2,1,0:T(8,128)(2,1)}, u32[]{:S(2)}) copy-start(bf16[8,256,512]{2,1,0:T(8,128)(2,1)} %maps_v.1) | copy-start | bytes 6291460
  22.6 20.2 %copy-start.1 = (bf16[8,256,256]{2,1,0:T(8,128)(2,1)S(1)}, bf16[8,256,256]{2,1,0:T(8,128)(2,1)}, u32[]{:S(2)}) copy-start(bf16[8,256,256]{2,1,0:T(8,128)(2,1)} %ups_v.1) | copy-start | bytes 3145732
  22.6 20.2 %copy-start.2 = (bf16[2,8,256,256]{3,2,1,0:T(8,128)(2,1)S(1)}, bf16[2,8,256,256]{3,2,1,0:T(8,128)(2,1)}, u32[]{:S(2)}) copy-start(bf16[2,8,256,256]{3,2,1,0:T(8,128)(2,1)} %fars_v.1) | copy-start | bytes 6291460
  22.6 20.2 %copy-start.3 = (f32[8,8,512]{2,1,0:T(8,128)S(1)}, f32[8,8,512]{2,1,0:T(8,128)}, u32[]{:S(2)}) copy-start(f32[8,8,512]{2,1,0:T(8,128)} %kry.3) | copy-start | bytes 393220
  22.6 20.2 %copy-start.5 = (bf16[7,32,512]{2,1,0:T(8,128)(2,1)S(1)}, bf16[7,32,512]{2,1,0:T(8,128)(2,1)}, u32[]{:S(2)}) copy-start(bf16[7,32,512]{2,1,0:T(8,128)(2,1)} %get-tuple-element.13.anw) | copy-start | bytes 688132
  22.6 20.2 %copy-start.6 = (f32[32,1,256]{2,1,0:T(1,128)S(1)}, f32[32,1,256]{2,1,0:T(1,128)}, u32[]{:S(2)}) copy-start(f32[32,1,256]{2,1,0:T(1,128)} %get-tuple-element.10.gmall) | copy-start | bytes 98308
  22.6 20.2 %copy-start.7 = (bf16[7,8,256]{2,1,0:T(8,128)(2,1)S(1)}, bf16[7,8,256]{2,1,0:T(8,128)(2,1)}, u32[]{:S(2)}) copy-start(bf16[7,8,256]{2,1,0:T(8,128)(2,1)} %get-tuple-element.9.momw) | copy-start | bytes 86020
  22.6 20.2 %copy-start.8 = (s32[8,16]{1,0:T(8,128)S(1)}, s32[8,16]{1,0:T(8,128)}, u32[]{:S(2)}) copy-start(s32[8,16]{1,0:T(8,128)} %llist.1) | copy-start | bytes 1540
  22.6 20.2 %copy-start.9 = (s32[8,16]{1,0:T(8,128)S(1)}, s32[8,16]{1,0:T(8,128)}, u32[]{:S(2)}) copy-start(s32[8,16]{1,0:T(8,128)} %lkind.1) | copy-start | bytes 1540
  22.6 20.2 %copy-start.10 = (s32[8]{0:T(128)S(1)}, s32[8]{0:T(128)}, u32[]{:S(2)}) copy-start(s32[8]{0:T(128)} %cnt.3) | copy-start | bytes 100
  22.7 20.2 %copy-start.11 = (s32[1,16]{1,0:T(1,128)S(1)}, s32[1,16]{1,0:T(1,128)}, u32[]{:S(2)}) copy-start(s32[1,16]{1,0:T(1,128)} %glist.1) | copy-start | bytes 196
  22.7 20.2 %copy-start.12 = (s32[1,16]{1,0:T(1,128)S(1)}, s32[1,16]{1,0:T(1,128)}, u32[]{:S(2)}) copy-start(s32[1,16]{1,0:T(1,128)} %gkind.1) | copy-start | bytes 196

commit v5 on v4

--- a/solution.py
+++ b/solution.py
@@ -124,6 +124,12 @@
     for c in range(local):
         counts = jnp.where(lane == c, cnt[c], counts)
     cntw[RADIUS] = counts
+    current = kry_v[...].astype(BF16)
+    density = jnp.zeros((local, panels), F32)
+    for c in range(local // 2):
+        copies[c].wait()
+        found = mm(current, binv_v[c], NT)
+        density = jnp.where(row_is(found.shape, c), found, density)
     pl.semaphore_wait(barrier, total - 1)
 
     def to_neighbours(ref, kind, rows=None):
@@ -149,9 +155,7 @@
 
     sent = to_neighbours(posw, 0) + to_neighbours(anw, 4, pl.ds(0, 3 * local)) + to_neighbours(cntw, 1)
     live = live_mask(cnt, (local, panels))
-    current = kry_v[...].astype(BF16)
-    density = jnp.zeros((local, panels), F32)
-    for c in range(local):
+    for c in range(local // 2, local):
         copies[c].wait()
         found = mm(current, binv_v[c], NT)
         density = jnp.where(row_is(found.shape, c), found, density)

time: 54.2 us -> 55.7 us (1.028)
  Pallas kernels: 48.8 us -> 50 us
    pallas_call x1, Pallas kernels: 9.39 us -> 12.1 us  [shards(): pl.pallas_call(functools.partial(finish_kernel, roles, devs), name='finis...]
    pallas_call x1, Pallas kernels: 20.1 us -> 18.6 us  [shards(): pl.pallas_call(near_kernel, name='near', cost_estimate=pl.CostEstimate(fl...]
where the time goes in v5:
time: 55.7 us; the launch traced here: 54.6 us
  Pallas kernels  50 us (90%)
  local copies, waits for them, and re-layouts  3.77 us (7%)
  between operations  0.86 us (2%)
    pallas_call x1, Pallas kernels, shards(): pl.pallas_call(functools.partial(source_kernel, roles, devs), name='sourc...  19.3 us
    pallas_call x1, Pallas kernels, shards(): pl.pallas_call(near_kernel, name='near', cost_estimate=pl.CostEstimate(fl...  18.6 us
    pallas_call x1, Pallas kernels, shards(): pl.pallas_call(functools.partial(finish_kernel, roles, devs), name='finis...  12.1 us
    unnamed x36, local copies, waits for them, and re-layouts  3.77 us

profile of v5, /device:TPU:0, one launch (start us, length us, event | category | flops | bytes accessed | tf_op | source)
XLA Modules:
  0.0 54.6 jit_solution(17405219391811603652)
XLA Ops:
  0.6 0.0 copy-start.14
  0.6 0.0 copy-start.16
  0.7 19.3 %sources.1 = (f32[7,3,8,512]{3,2,1,0:T(8,128)}, bf16[7,32,512]{2,1,0:T(8,128)(2,1)}, s32[7,1,128]{2,1,0:T(1,128)}, bf16[7,8,256]{2,1,0:T(8,128)(2,1)}, f32[32,1,256]{2,1,0:T(1,128)}) custom-call(s32[8]{0:T(128)} %cnt.3, f32[3,8,512]{2,1,0:T(8,128)} %bitcast.5, f32[3,8,512]{2,1,0:T(8,128)} %bitcast.6, f32[8,512]{1,0:T(8,128)} %area.1, f32[8,8,512]{2,1,0:T(8,128)} %kry.3, ...), custom_call_target="tpu_custom_call" | custom-call | tf_op jit(solution)/shard_map/sources/pallas_call | solution.py:467
  19.9 0.0 copy-done.14
  19.9 0.0 copy-done.16
  20.0 0.0 copy-start.4
  20.0 0.9 %copy-done.4 = bf16[7,32,512]{2,1,0:T(8,128)(2,1)S(1)} copy-done((bf16[7,32,512]{2,1,0:T(8,128)(2,1)S(1)}, bf16[7,32,512]{2,1,0:T(8,128)(2,1)}, u32[]{:S(2)}) %copy-start.4) | copy-done | bytes 229400
  20.9 0.0 copy-start.13
  20.9 1.0 %copy-done.13 = f32[7,3,8,512]{3,2,1,0:T(8,128)S(1)} copy-done((f32[7,3,8,512]{3,2,1,0:T(8,128)S(1)}, f32[7,3,8,512]{3,2,1,0:T(8,128)}, u32[]{:S(2)}) %copy-start.13) | copy-done | bytes 344088
  21.9 0.0 copy-start.15
  21.9 0.7 %copy-done.15 = s32[7,1,128]{2,1,0:T(1,128)S(1)} copy-done((s32[7,1,128]{2,1,0:T(1,128)S(1)}, s32[7,1,128]{2,1,0:T(1,128)}, u32[]{:S(2)}) %copy-start.15) | copy-done | bytes 3608
  22.6 0.0 copy-start
  22.6 0.0 copy-start.1
  22.6 0.0 copy-start.2
  22.6 0.0 copy-start.3
  22.6 0.0 copy-start.5
  22.6 0.0 copy-start.6
  22.6 0.0 copy-start.7
  22.6 0.0 copy-start.8
  22.6 0.0 copy-start.9
  22.6 0.0 copy-start.10
  22.6 0.0 copy-start.11
  22.6 0.0 copy-start.12
  22.7 18.6 %near.2 = f32[8,512]{1,0:T(8,128)S(1)} custom-call(s32[1]{0:T(128)} %bitcast.2.first, s32[8,6]{1,0:T(8,128)S(1)} %copy-done.14, s32[8]{0:T(128)S(1)} %copy-done.16, s32[7,1,128]{2,1,0:T(1,128)S(1)} %copy-done.15, f32[7,3,8,512]{3,2,1,0:T(8,128)S(1)} %copy-done.13, bf16[7,32,512]{2,1,0:T(8,128)(2,1)S(1)} %copy-done.4), custom_call_target="tpu_custom_call" | custom-call | flops 587202560 | bytes 1376256 | tf_op jit(solution)/shard_map/near/pallas_call | solution.py:509
  41.3 0.0 copy-done
  41.3 0.0 copy-done.1
  41.3 0.0 copy-done.2
  41.3 0.0 copy-done.3
  41.3 0.0 copy-done.5
  41.3 0.0 copy-done.6
  41.4 0.0 copy-done.7
  41.4 0.0 copy-done.8
  41.4 0.0 copy-done.9
  41.4 0.0 copy-done.10
  41.4 0.0 copy-done.11
  41.4 0.0 copy-done.12
  41.4 12.1 %finish.1 = (f32[8,512]{1,0:T(8,128)S(1)}, f32[1,9]{1,0:T(1,128)S(1)}) custom-call(s32[8]{0:T(128)S(1)} %copy-done.10, s32[1,16]{1,0:T(1,128)S(1)} %copy-done.11, s32[1,16]{1,0:T(1,128)S(1)} %copy-done.12, s32[8,16]{1,0:T(8,128)S(1)} %copy-done.8, s32[8,16]{1,0:T(8,128)S(1)} %copy-done.9, bf16[7,8,256]{2,1,0:T(8,128)(2,1)S(1)} %copy-done.7, ...), custom_call_target="tpu_custom_call" | custom-call | tf_op jit(solution)/shard_map/finish/pallas_call | solution.py:532
  53.5 0.6 %copy.19 = f32[8,512]{1,0:T(8,128)} copy(f32[8,512]{1,0:T(8,128)S(1)} %get-tuple-element.18) | data formatting | bytes 32768
  54.1 0.5 copy.20
Async XLA Ops:
  0.6 19.3 %copy-start.14 = (s32[8,6]{1,0:T(8,128)S(1)}, s32[8,6]{1,0:T(8,128)}, u32[]{:S(2)}) copy-start(s32[8,6]{1,0:T(8,128)} %near.3) | copy-start | bytes 580
  0.6 19.3 %copy-start.16 = (s32[8]{0:T(128)S(1)}, s32[8]{0:T(128)}, u32[]{:S(2)}) copy-start(s32[8]{0:T(128)} %used.1) | copy-start | bytes 100
  20.0 0.9 %copy-start.4 = (bf16[7,32,512]{2,1,0:T(8,128)(2,1)S(1)}, bf16[7,32,512]{2,1,0:T(8,128)(2,1)}, u32[]{:S(2)}) copy-start(bf16[7,32,512]{2,1,0:T(8,128)(2,1)} %get-tuple-element.13.anw) | copy-start | bytes 688132
  20.9 1.0 %copy-start.13 = (f32[7,3,8,512]{3,2,1,0:T(8,128)S(1)}, f32[7,3,8,512]{3,2,1,0:T(8,128)}, u32[]{:S(2)}) copy-start(f32[7,3,8,512]{3,2,1,0:T(8,128)} %get-tuple-element.12.posw) | copy-start | bytes 1032196
  21.9 0.7 %copy-start.15 = (s32[7,1,128]{2,1,0:T(1,128)S(1)}, s32[7,1,128]{2,1,0:T(1,128)}, u32[]{:S(2)}) copy-start(s32[7,1,128]{2,1,0:T(1,128)} %get-tuple-element.11.cntw) | copy-start | bytes 10756
  22.6 18.7 %copy-start = (bf16[8,256,512]{2,1,0:T(8,128)(2,1)S(1)}, bf16[8,256,512]{2,1,0:T(8,128)(2,1)}, u32[]{:S(2)}) copy-start(bf16[8,256,512]{2,1,0:T(8,128)(2,1)} %maps_v.1) | copy-start | bytes 6291460
  22.6 18.8 %copy-start.1 = (bf16[8,256,256]{2,1,0:T(8,128)(2,1)S(1)}, bf16[8,256,256]{2,1,0:T(8,128)(2,1)}, u32[]{:S(2)}) copy-start(bf16[8,256,256]{2,1,0:T(8,128)(2,1)} %ups_v.1) | copy-start | bytes 3145732
  22.6 18.8 %copy-start.2 = (bf16[2,8,256,256]{3,2,1,0:T(8,128)(2,1)S(1)}, bf16[2,8,256,256]{3,2,1,0:T(8,128)(2,1)}, u32[]{:S(2)}) copy-start(bf16[2,8,256,256]{3,2,1,0:T(8,128)(2,1)} %fars_v.1) | copy-start | bytes 6291460
  22.6 18.8 %copy-start.3 = (f32[8,8,512]{2,1,0:T(8,128)S(1)}, f32[8,8,512]{2,1,0:T(8,128)}, u32[]{:S(2)}) copy-start(f32[8,8,512]{2,1,0:T(8,128)} %kry.3) | copy-start | bytes 393220
  22.6 18.8 %copy-start.5 = (bf16[7,32,512]{2,1,0:T(8,128)(2,1)S(1)}, bf16[7,32,512]{2,1,0:T(8,128)(2,1)}, u32[]{:S(2)}) copy-start(bf16[7,32,512]{2,1,0:T(8,128)(2,1)} %get-tuple-element.13.anw) | copy-start | bytes 688132
  22.6 18.8 %copy-start.6 = (f32[32,1,256]{2,1,0:T(1,128)S(1)}, f32[32,1,256]{2,1,0:T(1,128)}, u32[]{:S(2)}) copy-start(f32[32,1,256]{2,1,0:T(1,128)} %get-tuple-element.10.gmall) | copy-start | bytes 98308
  22.6 18.8 %copy-start.7 = (bf16[7,8,256]{2,1,0:T(8,128)(2,1)S(1)}, bf16[7,8,256]{2,1,0:T(8,128)(2,1)}, u32[]{:S(2)}) copy-start(bf16[7,8,256]{2,1,0:T(8,128)(2,1)} %get-tuple-element.9.momw) | copy-start | bytes 86020
  22.6 18.8 %copy-start.8 = (s32[8,16]{1,0:T(8,128)S(1)}, s32[8,16]{1,0:T(8,128)}, u32[]{:S(2)}) copy-start(s32[8,16]{1,0:T(8,128)} %llist.1) | copy-start | bytes 1540
  22.6 18.8 %copy-start.9 = (s32[8,16]{1,0:T(8,128)S(1)}, s32[8,16]{1,0:T(8,128)}, u32[]{:S(2)}) copy-start(s32[8,16]{1,0:T(8,128)} %lkind.1) | copy-start | bytes 1540
  22.6 18.8 %copy-start.10 = (s32[8]{0:T(128)S(1)}, s32[8]{0:T(128)}, u32[]{:S(2)}) copy-start(s32[8]{0:T(128)} %cnt.3) | copy-start | bytes 100
  22.6 18.8 %copy-start.11 = (s32[1,16]{1,0:T(1,128)S(1)}, s32[1,16]{1,0:T(1,128)}, u32[]{:S(2)}) copy-start(s32[1,16]{1,0:T(1,128)} %glist.1) | copy-start | bytes 196
  22.6 18.8 %copy-start.12 = (s32[1,16]{1,0:T(1,128)S(1)}, s32[1,16]{1,0:T(1,128)}, u32[]{:S(2)}) copy-start(s32[1,16]{1,0:T(1,128)} %gkind.1) | copy-start | bytes 196
